TPU v7x, 32 devices: a whole 2x2x4 slice. The times are simulated.
32 devices in a mesh: seq: 16 (over z, x, core), wshard: 2 (over y).
Axes of the slice: x: 2, y: 2, z: 4, core: 2. Of those that a mesh axis runs over, the one named last changes fastest.
Arguments:
- inputs: bfloat16 [8192, 640], P(('seq', 'wshard')), may hold values from -6 to 6
- doc_ids: int32 [8192], P(('seq', 'wshard')), may hold values from 0 to 2, never falling along the last dimension, each value on 1 to 4096 neighbouring positions
- w_query: bfloat16 [640, 1024], P('wshard'), may hold values from -0.25 to 0.25
- w_key: bfloat16 [640, 256], P('wshard'), may hold values from -0.25 to 0.25
- w_value: bfloat16 [640, 256], P('wshard'), may hold values from -0.25 to 0.25
- w_out: bfloat16 [1024, 640], P('wshard'), may hold values from -0.1875 to 0.1875
- w_gate: bfloat16 [640, 2048], P('wshard'), may hold values from -0.25 to 0.25
- w_up: bfloat16 [640, 2048], P('wshard'), may hold values from -0.25 to 0.25
- w_down: bfloat16 [2048, 640], P('wshard'), may hold values from -0.125 to 0.125
- gain_in: bfloat16 [640], P('wshard'), may hold values from -0.5 to 1
- gain_attn_post: bfloat16 [640], P('wshard'), may hold values from -0.5 to 1
- gain_ff_pre: bfloat16 [640], P('wshard'), may hold values from -0.5 to 1
- gain_ff_post: bfloat16 [640], P('wshard'), may hold values from -0.5 to 1
- gain_query: bfloat16 [256], P('wshard'), may hold values from -0.5 to 1
- gain_key: bfloat16 [256], P('wshard'), may hold values from -0.5 to 1
- cotangent: bfloat16 [8192, 640], P(('seq', 'wshard')), may hold values from -6 to 6
Outputs:
- layer_out: bfloat16 [8192, 640], P(('seq', 'wshard'))
- grad_inputs: float32 [8192, 640], P(('seq', 'wshard'))
- grad_w_query: float32 [640, 1024], P('wshard')
- grad_w_key: float32 [640, 256], P('wshard')
- grad_w_value: float32 [640, 256], P('wshard')
- grad_w_out: float32 [1024, 640], P('wshard')
- grad_w_gate: float32 [640, 2048], P('wshard')
- grad_w_up: float32 [640, 2048], P('wshard')
- grad_w_down: float32 [2048, 640], P('wshard')
- grad_gain_in: float32 [640], P('wshard')
- grad_gain_attn_post: float32 [640], P('wshard')
- grad_gain_ff_pre: float32 [640], P('wshard')
- grad_gain_ff_post: float32 [640], P('wshard')
- grad_gain_query: float32 [256], P('wshard')
- grad_gain_key: float32 [256], P('wshard')
Inputs may be any that keep to these rules, and one draw needn't show every extreme that they name: `doc_ids`: document numbers never fall along the token stream; every document has 1 to 4096 tokens, one exactly 4096.
All inputs are finite; a program needn't handle non-finite values.
Results may differ from a plain program's by a relative error of at most 0.025.
Values may be sent and summed in bfloat16 or wider, within the bound.
A program may use at most 128 MiB of HBM per device.

v0:
```python
import functools

import jax
import jax.numpy as jnp
from jax import lax
from jax.experimental import pallas as pl
from jax.experimental.pallas import tpu as pltpu
from jax.sharding import PartitionSpec as P

WINDOW = 512


NORM_EPSILON = 1e-06
ROPE_BASE = 10000.0
MASK_FLOOR = -1e30


def from_behind(array, axis, by):
    count = lax.axis_size(axis)
    pairs = [(i, i + by) for i in range(count) if 0 <= i + by < count]
    return lax.ppermute(array, axis, pairs)


def rms_gain(tensor, gain_vec):
    factor = lax.rsqrt(jnp.mean(tensor * tensor, axis=-1, keepdims=True) + NORM_EPSILON)
    return tensor * factor * (1.0 + gain_vec)


def rope_tables(positions, head_width):
    half_width = head_width // 2
    exponent = jnp.arange(half_width, dtype=jnp.float32) * (2.0 / head_width)
    inverse = jnp.exp(-jnp.log(ROPE_BASE) * exponent)
    angles = positions.astype(jnp.float32)[:, None] * inverse[None, :]
    return (jnp.cos(angles), jnp.sin(angles))


def norm_rope(tensor, gain_vec, cos_table, sin_table):
    normed = rms_gain(tensor, gain_vec)
    half_width = tensor.shape[-1] // 2
    front_part = normed[..., :half_width]
    back_part = normed[..., half_width:]
    cos_rows = cos_table[:, None, :]
    sin_rows = sin_table[:, None, :]
    return jnp.concatenate(
        [
            front_part * cos_rows - back_part * sin_rows,
            back_part * cos_rows + front_part * sin_rows,
        ],
        axis=-1,
    )


def geglu(gate_pre, up_pre):
    return jax.nn.gelu(gate_pre, approximate=True) * up_pre


def window_mask(query_pos, key_pos, query_doc, key_doc):
    distance = query_pos[:, None] - key_pos[None, :]
    return (
        (distance >= 0)
        & (distance < WINDOW)
        & (key_pos[None, :] >= 0)
        & (query_doc[:, None] == key_doc[None, :])
    )


def masked_scores(queries, all_keys, allowed, score_scale):
    scores = (
        jnp.einsum("qhd,kd->hqk", queries, all_keys, preferred_element_type=jnp.float32)
        * score_scale
    )
    return jnp.where(allowed[None], scores, MASK_FLOOR)


def weight_grad(left_rows, right_rows):
    return jnp.einsum("tc,tf->cf", left_rows, right_rows, preferred_element_type=jnp.float32)


MESH = pl.DeviceIdType.MESH
LANES = 128


def coordinates():
    seq = lax.axis_index("seq")
    return lax.rem(seq // 2, 2), lax.rem(seq, 2), seq // 4, lax.axis_index("wshard")


def device(x, core, z, y):
    return ((z * 2 + x) * 2 + core, y)


def greet(partners):
    barrier = pltpu.get_barrier_semaphore()
    for partner in partners:
        pl.semaphore_signal(barrier, inc=1, device_id=partner, device_id_type=MESH)
    pl.semaphore_wait(barrier, len(partners))


def remote(src, dst, send, recv, target):
    return pltpu.make_async_remote_copy(
        src_ref=src, dst_ref=dst, send_sem=send, recv_sem=recv,
        device_id=target, device_id_type=MESH,
    )


def gather_kernel(count, *refs):
    shards, fulls = refs[:count], refs[count : 2 * count]
    own_sem, send_sems, recv_sems = refs[2 * count :]
    x, core, z, y = coordinates()
    sibling = device(x, 1 - core, z, y)
    beside = device(1 - x, core, z, y)
    across = device(x, core, z, 1 - y)
    greet([sibling, beside, across])

    def local(i):
        rows = shards[i].shape[0]
        return pltpu.make_async_copy(
            shards[i], fulls[i].at[pl.ds(y * rows, rows)], own_sem.at[i]
        )

    def first(i):
        rows = shards[i].shape[0]
        part = rows if i == count - 1 else rows // 4
        at = 0 if i == count - 1 else (core * 2 + x) * part
        return remote(
            shards[i].at[pl.ds(at, part)], fulls[i].at[pl.ds(y * rows + at, part)],
            send_sems.at[0, i], recv_sems.at[0, i], across,
        )

    def second(i):
        rows = shards[i].shape[0]
        part = rows // 4
        block = fulls[i].at[pl.ds((1 - y) * rows + (core * 2 + x) * part, part)]
        return remote(block, block, send_sems.at[1, i], recv_sems.at[1, i], beside)

    def third(i):
        rows = shards[i].shape[0]
        part = rows // 2
        block = fulls[i].at[pl.ds((1 - y) * rows + core * part, part)]
        return remote(block, block, send_sems.at[2, i], recv_sems.at[2, i], sibling)

    order = [count - 1] + list(range(count - 1))
    for i in order:
        first(i).start()
    for i in range(count):
        local(i).start()
    first(count - 1).wait_recv()
    big = count - 1
    for step in range(big + 1):
        if step < big:
            first(step).wait_recv()
            second(step).start()
        if step >= 1:
            second(step - 1).wait_recv()
            third(step - 1).start()
    for i in range(big):
        third(i).wait_recv()
    for i in range(count):
        local(i).wait()
        first(i).wait_send()
    for i in range(big):
        second(i).wait_send()
        third(i).wait_send()


def gather_weights(shards):
    count = len(shards)
    return pl.pallas_call(
        functools.partial(gather_kernel, count),
        out_shape=[jax.ShapeDtypeStruct((2 * s.shape[0],) + s.shape[1:], s.dtype) for s in shards],
        in_specs=[pl.BlockSpec(memory_space=pl.ANY)] * count,
        out_specs=[pl.BlockSpec(memory_space=pltpu.VMEM)] * count,
        scratch_shapes=[
            pltpu.SemaphoreType.DMA((count,)),
            pltpu.SemaphoreType.DMA((3, count)),
            pltpu.SemaphoreType.DMA((3, count)),
        ],
        compiler_params=pltpu.CompilerParams(
            collective_id=1, has_side_effects=True, vmem_limit_bytes=58 * 2**20
        ),
        name="gather_weights",
    )(*shards)


def term_groups(lefts, rights, depth):
    groups = []
    for left, right in zip(lefts, rights):
        columns = right.shape[1]
        by_columns = columns % (depth * LANES) == 0
        piece = lefts[0].shape[1] // 8 * LANES
        if by_columns:
            chunks = columns // (depth * LANES)
        else:
            chunks = left.shape[1] * columns // (8 * depth * piece)
        groups.append((left, right, by_columns, chunks))
    return groups


def reduce_kernel(
    count, *refs
):
    reduce_body(refs[:count], refs[count : 2 * count], *refs[2 * count :])


def token_dot(left, right):
    return lax.dot_general(
        left, right, (((0,), (0,)), ((), ())), preferred_element_type=jnp.float32
    ).astype(jnp.bfloat16)


def reduce_body(
    lefts, rights, gains, out, gains_out,
    terms, from_core, from_across, from_beside, from_line, gain_in,
    send_core, recv_core, send_across, recv_across, send_beside, recv_beside,
    send_line, recv_line, send_zline, recv_zline, send_xback, recv_xback,
    send_back, recv_back, send_gain, recv_gain,
):
    chunks = terms.shape[0]
    depth = terms.shape[4]
    x, core, z, y = coordinates()
    sibling = device(x, 1 - core, z, y)
    beside = device(1 - x, core, z, y)
    across = device(x, core, z, 1 - y)
    line = [device(x, core, lax.rem(z + d, depth), y) for d in range(1, depth)]
    greet([sibling, beside, across] + line)

    def to_core(c):
        return remote(terms.at[c, 1 - core], from_core.at[c], send_core.at[c], recv_core.at[c], sibling)

    def to_across(c):
        return remote(
            from_core.at[c, 1 - y], from_across.at[c], send_across.at[c], recv_across.at[c], across
        )

    def to_beside(c):
        return remote(
            from_across.at[c, 1 - x], from_beside.at[c], send_beside.at[c], recv_beside.at[c], beside
        )

    def to_line(c, d):
        return remote(
            from_beside.at[c, lax.rem(z + d, depth)], from_line.at[c, d - 1],
            send_line.at[c, d - 1], recv_line.at[c, d - 1], line[d - 1],
        )

    def along_line(c, d):
        block = out.at[c, core, x, z]
        return remote(block, block, send_zline.at[c, d - 1], recv_zline.at[c, d - 1], line[d - 1])

    def along_line_arrival(c, d):
        block = out.at[c, core, x, lax.rem(z + depth - d, depth)]
        return remote(block, block, send_zline.at[c, d - 1], recv_zline.at[c, d - 1], line[d - 1])

    def back_beside(c, side):
        block = out.at[c, core, side]
        return remote(block, block, send_xback.at[c], recv_xback.at[c], beside)

    def back_core(c, side):
        block = out.at[c, side]
        return remote(block, block, send_back.at[c], recv_back.at[c], sibling)

    def gain_copy(step):
        target = ([sibling, across, beside] + line)[step]
        src = gains if step == 0 else gains_out.at[min(step, 3) - 1]
        return remote(src, gain_in.at[step], send_gain.at[step], recv_gain.at[step], target)

    def add(a, b):
        return (a.astype(jnp.float32) + b.astype(jnp.float32)).astype(jnp.bfloat16)

    gain_copy(0).start()
    piece_rows = terms.shape[5]

    def make_columns(left, right, at, c):
        width = depth * LANES
        block = token_dot(left[...], right[:, pl.ds(pl.multiple_of(at * width, width), width)])
        for side in range(2):
            for own in range(2):
                for across_x in range(2):
                    low = ((side * 2 + own) * 2 + across_x) * piece_rows
                    for place in range(depth):
                        terms[c, own, side, across_x, place] = block[
                            low : low + piece_rows, place * LANES : (place + 1) * LANES
                        ]

    def make_rows(left, right, at, c, parts):
        rows, tiles = left.shape[1] // (2 * parts), right.shape[1] // LANES
        high = rows // (4 * depth)
        for side in range(2):
            start = pl.multiple_of((side * parts + at) * rows, rows)
            block = token_dot(left[:, pl.ds(start, rows)], right[...])
            for own in range(2):
                for across_x in range(2):
                    for place in range(depth):
                        low = ((own * 2 + across_x) * depth + place) * high
                        for tile in range(tiles):
                            terms[
                                c, own, side, across_x, place, tile * high : (tile + 1) * high
                            ] = block[low : low + high, tile * LANES : (tile + 1) * LANES]

    def make(t):
        start = 0
        for left, right, by_columns, parts in term_groups(lefts, rights, depth):
            @pl.when((t >= start) & (t < start + parts))
            def _(left=left, right=right, by_columns=by_columns, parts=parts, start=start):
                if by_columns:
                    make_columns(left, right, t - start, t)
                else:
                    make_rows(left, right, t - start, t, parts)
            start += parts
        to_core(t).start()

    def stage(at, action):
        @pl.when((at >= 0) & (at < chunks))
        def _():
            action(at)

    def after_core(c):
        to_core(c).wait_recv()
        from_core[c, 1 - y] = add(from_core[c, 1 - y], terms[c, core, 1 - y])
        to_across(c).start()
        from_core[c, y] = add(from_core[c, y], terms[c, core, y])

    def after_across(c):
        to_across(c).wait_recv()
        from_across[c, 1 - x] = add(from_across[c, 1 - x], from_core[c, y, 1 - x])
        to_beside(c).start()
        from_across[c, x] = add(from_across[c, x], from_core[c, y, x])

    def after_beside(c):
        to_beside(c).wait_recv()
        from_beside[c] = add(from_beside[c], from_across[c, x])
        for d in range(1, depth):
            to_line(c, d).start()

    def after_line(c):
        total = from_beside[c, z].astype(jnp.float32)
        for d in range(1, depth):
            to_line(c, d).wait_recv()
            total = total + from_line[c, d - 1].astype(jnp.float32)
        out[c, core, x, z] = total.astype(jnp.bfloat16)
        for d in range(1, depth):
            along_line(c, d).start()

    def after_zline(c):
        for d in range(1, depth):
            along_line_arrival(c, d).wait_recv()
        back_beside(c, x).start()

    def after_xback(c):
        back_beside(c, 1 - x).wait_recv()
        back_core(c, core).start()

    actions = [make, after_core, after_across, after_beside, after_line, after_zline, after_xback]

    @pl.loop(0, chunks + len(actions) - 1)
    def _(t):
        for lag, action in enumerate(actions):
            stage(t - lag, action)
        for step in range(3):
            @pl.when(t == step + 1)
            def _():
                gain_copy(step).wait_recv()
                before = gains[...] if step == 0 else gains_out[step - 1]
                gains_out[step] = before + gain_in[step]
                if step < 2:
                    gain_copy(step + 1).start()
                else:
                    for d in range(1, depth):
                        gain_copy(2 + d).start()

    total = gains_out[2]
    for d in range(1, depth):
        gain_copy(2 + d).wait_recv()
        total = total + gain_in[2 + d]
    gains_out[3] = total
    for step in range(2 + depth):
        gain_copy(step).wait_send()

    @pl.loop(0, chunks)
    def _(c):
        back_core(c, 1 - core).wait_recv()
        to_core(c).wait_send()
        to_across(c).wait_send()
        to_beside(c).wait_send()
        for d in range(1, depth):
            to_line(c, d).wait_send()
            along_line(c, d).wait_send()
        back_beside(c, x).wait_send()
        back_core(c, core).wait_send()


def reduce_terms(lefts, rights, gains):
    depth = lax.axis_size("seq") // 4
    groups = term_groups(lefts, rights, depth)
    chunks = sum(group[3] for group in groups)
    piece = (lefts[0].shape[1] // 8, LANES)
    dma = pltpu.SemaphoreType.DMA
    vmem = pl.BlockSpec(memory_space=pltpu.VMEM)
    pair = [dma((chunks,)), dma((chunks,))]
    lines = [dma((chunks, depth - 1)), dma((chunks, depth - 1))]
    steps = 2 + depth
    return pl.pallas_call(
        functools.partial(reduce_kernel, len(lefts)),
        out_shape=[
            jax.ShapeDtypeStruct((chunks, 2, 2, depth) + piece, jnp.bfloat16),
            jax.ShapeDtypeStruct((4,) + gains.shape, jnp.float32),
        ],
        in_specs=[vmem] * (2 * len(lefts) + 1),
        out_specs=[vmem, vmem],
        scratch_shapes=[
            pltpu.VMEM((chunks, 2, 2, 2, depth) + piece, jnp.bfloat16),
            pltpu.VMEM((chunks, 2, 2, depth) + piece, jnp.bfloat16),
            pltpu.VMEM((chunks, 2, depth) + piece, jnp.bfloat16),
            pltpu.VMEM((chunks, depth) + piece, jnp.bfloat16),
            pltpu.VMEM((chunks, depth - 1) + piece, jnp.bfloat16),
            pltpu.VMEM((steps,) + gains.shape, jnp.float32),
        ]
        + pair + pair + pair + lines + lines + pair + pair
        + [dma((steps,)), dma((steps,))],
        compiler_params=pltpu.CompilerParams(
            collective_id=2, has_side_effects=True, vmem_limit_bytes=56 * 2**20
        ),
        name="reduce_terms",
    )(*lefts, *rights, gains)


def unpack_kernel(plan, summed, *outs):
    c = pl.program_id(0)
    depth, rows = summed.shape[3], summed.shape[4]
    for outputs, by_columns, start, parts in plan:
        @pl.when((c >= start) & (c < start + parts))
        def _(outputs=outputs, by_columns=by_columns):
            for core in range(2):
                for x in range(2):
                    for z in range(depth):
                        piece = summed[0, core, x, z].astype(jnp.float32)
                        if by_columns:
                            low = (core * 2 + x) * rows
                            ref, column = outputs[0], z * LANES
                            width = outs[ref].shape[1]
                            ref, column = ref + column // width, column % width
                            outs[ref][low : low + rows, column : column + LANES] = piece
                        else:
                            ref = outs[outputs[0]]
                            tiles = ref.shape[1] // LANES
                            high = rows // tiles
                            low = ((core * 2 + x) * depth + z) * high
                            for tile in range(tiles):
                                ref[low : low + high, tile * LANES : (tile + 1) * LANES] = piece[
                                    tile * high : (tile + 1) * high
                                ]


def unpack(summed, shapes):
    chunks, _, _, depth, rows, lanes = summed.shape
    width = depth * lanes
    plan, shaped, specs, start, index = [], [], [], 0, 0
    while index < len(shapes):
        high, wide = shapes[index]
        together = max(1, width // wide) if wide <= width and width % wide == 0 else 1
        by_columns = (wide * together) % width == 0
        if by_columns:
            parts = wide * together // width
            block = (high, min(wide, width))
        else:
            parts = high * wide // (4 * depth * rows * lanes)
            block = (high // parts, wide)
        plan.append((list(range(index, index + together)), by_columns, start, parts))

        def place(c, start=start, parts=parts, by_columns=by_columns):
            at = jnp.clip(c - start, 0, parts - 1)
            return (0, at) if by_columns else (at, 0)

        for k in range(together):
            shaped.append(jax.ShapeDtypeStruct(shapes[index + k], jnp.float32))
            specs.append(pl.BlockSpec(block, place))
        start += parts
        index += together
    return pl.pallas_call(
        functools.partial(unpack_kernel, plan),
        grid=(chunks,),
        out_shape=shaped,
        in_specs=[pl.BlockSpec((1,) + summed.shape[1:], lambda c: (c, 0, 0, 0, 0, 0))],
        out_specs=specs,
        name="unpack",
    )(summed)


def shift_kernel(count, hops, step, *refs):
    arrays, outs = refs[:count], refs[count : 2 * count]
    send_sems, recv_sems = refs[2 * count :]
    width = lax.axis_size("wshard")
    total = lax.axis_size("seq") * width
    me = lax.axis_index("seq") * width + lax.axis_index("wshard")
    barrier = pltpu.get_barrier_semaphore()
    offsets = [d for d in range(-hops, hops + 1) if d != 0]

    def there(offset):
        return (me + offset >= 0) & (me + offset < total)

    def target(offset):
        place = lax.rem(me + offset + total, total)
        return (place // width, lax.rem(place, width))

    for offset in offsets:
        pl.semaphore_signal(
            barrier, inc=1, device_id=target(offset), device_id_type=MESH
        )
    pl.semaphore_wait(barrier, len(offsets))

    def copy(k, d):
        source = arrays[k] if step > 0 else arrays[k].at[hops - d]
        return remote(
            source, outs[k].at[d - 1], send_sems.at[k, d - 1], recv_sems.at[k, d - 1],
            target(step * d),
        )

    for d in range(1, hops + 1):
        @pl.when(there(step * d))
        def _():
            for k in range(count):
                copy(k, d).start()
    for d in range(1, hops + 1):
        @pl.when(there(-step * d))
        def _():
            for k in range(count):
                copy(k, d).wait_recv()

        @pl.when(jnp.logical_not(there(-step * d)))
        def _():
            for k in range(count):
                outs[k][d - 1] = jnp.zeros(outs[k].shape[1:], outs[k].dtype)
    for d in range(1, hops + 1):
        @pl.when(there(step * d))
        def _():
            for k in range(count):
                copy(k, d).wait_send()


def shift(arrays, hops, step, name, collective_id):
    count = len(arrays)
    vmem = pl.BlockSpec(memory_space=pltpu.VMEM)
    shapes = [a.shape if step > 0 else a.shape[1:] for a in arrays]
    return pl.pallas_call(
        functools.partial(shift_kernel, count, hops, step),
        out_shape=[
            jax.ShapeDtypeStruct((hops,) + s, a.dtype) for s, a in zip(shapes, arrays)
        ],
        in_specs=[vmem] * count,
        out_specs=[vmem] * count,
        scratch_shapes=[
            pltpu.SemaphoreType.DMA((count, hops)),
            pltpu.SemaphoreType.DMA((count, hops)),
        ],
        compiler_params=pltpu.CompilerParams(collective_id=collective_id, has_side_effects=True),
        name=name,
    )(*arrays)


def per_device(
    inputs,
    doc_ids,
    w_query,
    w_key,
    w_value,
    w_out,
    w_gate,
    w_up,
    w_down,
    gain_in,
    gain_attn_post,
    gain_ff_pre,
    gain_ff_post,
    gain_query,
    gain_key,
    cotangent,
):
    small = (gain_in, gain_attn_post, gain_ff_pre, gain_ff_post, gain_query, gain_key)
    small_shard = jnp.concatenate(small).astype(jnp.float32).reshape(1, -1, LANES)
    gathered = gather_weights(
        (w_query, w_key, w_value, w_out, w_gate, w_up, w_down, small_shard)
    )
    full_query, full_key, full_value, full_out, full_gate, full_up, full_down = gathered[:7]
    small_full = gathered[7].reshape(2, -1)
    starts = [0]
    for vec in small:
        starts.append(starts[-1] + vec.shape[0])
    in_gain, attn_post_gain, ff_pre_gain, ff_post_gain, query_gain, key_gain = [
        small_full[:, low:high].reshape(-1) for low, high in zip(starts[:-1], starts[1:])
    ]
    row_count = inputs.shape[0]
    head_dim = full_key.shape[1]
    head_count = full_query.shape[1] // head_dim
    score_scale = head_dim ** (-0.5)
    start_row = lax.axis_index(("seq", "wshard")) * row_count
    query_pos = start_row + jnp.arange(row_count, dtype=jnp.int32)
    cos_table, sin_table = rope_tables(query_pos, head_dim)
    x_float = inputs.astype(jnp.float32)
    normed_in = rms_gain(x_float, in_gain).astype(jnp.bfloat16)
    query_raw = jnp.dot(normed_in, full_query, preferred_element_type=jnp.float32).reshape(
        row_count, head_count, head_dim
    )
    key_raw = jnp.dot(normed_in, full_key, preferred_element_type=jnp.float32)[:, None, :]
    values = jnp.dot(normed_in, full_value, preferred_element_type=jnp.float32).astype(jnp.bfloat16)
    queries = norm_rope(query_raw, query_gain, cos_table, sin_table).astype(jnp.bfloat16)
    key_rot = norm_rope(key_raw, key_gain, cos_table, sin_table)[:, 0].astype(jnp.bfloat16)
    sent_rows = min(WINDOW, row_count)
    hop_count = WINDOW // sent_rows
    arrived = shift(
        (key_rot, values, doc_ids.reshape(-1, LANES)), hop_count, 1, "shift_on", 3
    )
    order = range(hop_count - 1, -1, -1)
    halo_keys = [arrived[0][i] for i in order]
    halo_values = [arrived[1][i] for i in order]
    halo_docs = [arrived[2][i].reshape(-1) for i in order]
    all_keys = jnp.concatenate(halo_keys + [key_rot], 0)
    all_values = jnp.concatenate(halo_values + [values], 0)
    all_docs = jnp.concatenate(halo_docs + [doc_ids], 0)
    key_pos = start_row - WINDOW + jnp.arange(WINDOW + row_count, dtype=jnp.int32)
    allowed = window_mask(query_pos, key_pos, doc_ids, all_docs)
    scores = masked_scores(queries, all_keys, allowed, score_scale)
    row_peak = jnp.max(scores, axis=-1, keepdims=True)
    row_total = jnp.sum(
        jnp.where(allowed[None], jnp.exp(scores - row_peak), 0.0), axis=-1, keepdims=True
    )
    log_total = row_peak + jnp.log(row_total)
    soft = jnp.where(allowed[None], jnp.exp(scores - log_total), 0.0).astype(jnp.bfloat16)
    attended = jnp.einsum("hqk,kd->qhd", soft, all_values, preferred_element_type=jnp.float32)
    attended = attended.reshape(row_count, head_count * head_dim).astype(jnp.bfloat16)
    attn_proj = jnp.dot(attended, full_out, preferred_element_type=jnp.float32)
    resid = x_float + rms_gain(attn_proj, attn_post_gain)
    normed_ff = rms_gain(resid, ff_pre_gain).astype(jnp.bfloat16)
    gate_pre = jnp.dot(normed_ff, full_gate, preferred_element_type=jnp.float32)
    up_pre = jnp.dot(normed_ff, full_up, preferred_element_type=jnp.float32)
    hidden = geglu(gate_pre, up_pre).astype(jnp.bfloat16)
    ff_proj = jnp.dot(hidden, full_down, preferred_element_type=jnp.float32)
    layer_out = (resid + rms_gain(ff_proj, ff_post_gain)).astype(jnp.bfloat16)
    grad_top = cotangent.astype(jnp.float32)
    _, pullback = jax.vjp(rms_gain, ff_proj, ff_post_gain)
    grad_ff_proj, grad_gain_ff_post = pullback(grad_top)
    grad_ff_proj = grad_ff_proj.astype(jnp.bfloat16)
    grad_hidden = lax.dot_general(
        grad_ff_proj, full_down, (((1,), (1,)), ((), ())), preferred_element_type=jnp.float32
    )
    _, pullback = jax.vjp(geglu, gate_pre, up_pre)
    grad_gate, grad_up = pullback(grad_hidden)
    grad_gate = grad_gate.astype(jnp.bfloat16)
    grad_up = grad_up.astype(jnp.bfloat16)
    grad_normed_ff = lax.dot_general(
        grad_gate, full_gate, (((1,), (1,)), ((), ())), preferred_element_type=jnp.float32
    )
    grad_normed_ff = grad_normed_ff + lax.dot_general(
        grad_up, full_up, (((1,), (1,)), ((), ())), preferred_element_type=jnp.float32
    )
    _, pullback = jax.vjp(rms_gain, resid, ff_pre_gain)
    grad_resid_part, grad_gain_ff_pre = pullback(grad_normed_ff)
    grad_resid = grad_top + grad_resid_part
    _, pullback = jax.vjp(rms_gain, attn_proj, attn_post_gain)
    grad_attn_proj, grad_gain_attn_post = pullback(grad_resid)
    grad_attn_proj = grad_attn_proj.astype(jnp.bfloat16)
    grad_attended = lax.dot_general(
        grad_attn_proj, full_out, (((1,), (1,)), ((), ())), preferred_element_type=jnp.float32
    ).astype(jnp.bfloat16)
    grad_heads = grad_attended.reshape(row_count, head_count, head_dim)
    again_scores = masked_scores(queries, all_keys, allowed, score_scale)
    probs = jnp.where(allowed[None], jnp.exp(again_scores - log_total), 0.0)
    grad_soft = jnp.einsum(
        "qhd,kd->hqk", grad_heads, all_values, preferred_element_type=jnp.float32
    )
    row_inner = jnp.sum(probs * grad_soft, axis=-1, keepdims=True)
    grad_score = (probs * (grad_soft - row_inner) * score_scale).astype(jnp.bfloat16)
    grad_queries = jnp.einsum(
        "hqk,kd->qhd", grad_score, all_keys, preferred_element_type=jnp.float32
    )
    grad_keys_all = jnp.einsum(
        "hqk,qhd->kd", grad_score, queries, preferred_element_type=jnp.float32
    )
    grad_values_all = jnp.einsum(
        "hqk,qhd->kd", probs.astype(jnp.bfloat16), grad_heads, preferred_element_type=jnp.float32
    )
    pieces = (hop_count, sent_rows, head_dim)
    returned = shift(
        (
            grad_keys_all[:WINDOW].astype(jnp.bfloat16).reshape(pieces),
            grad_values_all[:WINDOW].astype(jnp.bfloat16).reshape(pieces),
        ),
        hop_count, -1, "shift_back", 4,
    )
    back_keys, back_values = [jnp.sum(r.astype(jnp.float32), axis=0) for r in returned]
    own_keys = grad_keys_all[WINDOW:]
    own_values = grad_values_all[WINDOW:]
    split_row = row_count - sent_rows
    grad_keys = jnp.concatenate([own_keys[:split_row], own_keys + back_keys], 0)
    grad_values = jnp.concatenate([own_values[:split_row], own_values + back_values], 0).astype(
        jnp.bfloat16
    )

    def query_path(tensor, gain_vec):
        return norm_rope(tensor, gain_vec, cos_table, sin_table)

    _, pullback = jax.vjp(query_path, query_raw, query_gain)
    grad_query_raw, grad_gain_query = pullback(grad_queries)
    _, pullback = jax.vjp(query_path, key_raw, key_gain)
    grad_key_raw, grad_gain_key = pullback(grad_keys[:, None, :])
    grad_query_raw = grad_query_raw.reshape(row_count, head_count * head_dim).astype(jnp.bfloat16)
    grad_key_raw = grad_key_raw[:, 0].astype(jnp.bfloat16)
    grad_normed_in = lax.dot_general(
        grad_query_raw, full_query, (((1,), (1,)), ((), ())), preferred_element_type=jnp.float32
    )
    grad_normed_in = grad_normed_in + lax.dot_general(
        grad_key_raw, full_key, (((1,), (1,)), ((), ())), preferred_element_type=jnp.float32
    )
    grad_normed_in = grad_normed_in + lax.dot_general(
        grad_values, full_value, (((1,), (1,)), ((), ())), preferred_element_type=jnp.float32
    )
    _, pullback = jax.vjp(rms_gain, x_float, in_gain)
    grad_input_part, grad_gain_in = pullback(grad_normed_in)
    grad_inputs = grad_resid + grad_input_part
    keys_values = jnp.concatenate([grad_key_raw, grad_values], axis=1)
    lefts = (normed_ff, normed_ff, hidden, normed_in, normed_in, attended)
    rights = (grad_gate, grad_up, grad_ff_proj, grad_query_raw, keys_values, grad_attn_proj)
    gain_terms = (
        grad_gain_in, grad_gain_attn_post, grad_gain_ff_pre, grad_gain_ff_post,
        grad_gain_query, grad_gain_key,
    )
    gain_rows = jnp.concatenate(gain_terms).astype(jnp.bfloat16).astype(jnp.float32)
    summed, gain_sums = reduce_terms(lefts, rights, gain_rows.reshape(-1, LANES))
    sum_gate, sum_up, sum_down, sum_query, sum_key, sum_value, sum_out = unpack(
        summed, [w.shape for w in (w_gate, w_up, w_down, w_query, w_key, w_value, w_out)]
    )
    me = lax.axis_index("wshard")
    gain_sums = gain_sums[3].reshape(-1)
    gain_outs = []
    start = 0
    for term in gain_terms:
        half = term.shape[0] // 2
        gain_outs.append(lax.dynamic_slice_in_dim(gain_sums, start + me * half, half))
        start += term.shape[0]
    return (
        layer_out, grad_inputs, sum_query, sum_key, sum_value, sum_out, sum_gate, sum_up, sum_down,
    ) + tuple(gain_outs)


def per_device_general(
    inputs,
    doc_ids,
    w_query,
    w_key,
    w_value,
    w_out,
    w_gate,
    w_up,
    w_down,
    gain_in,
    gain_attn_post,
    gain_ff_pre,
    gain_ff_post,
    gain_query,
    gain_key,
    cotangent,
):
    gathered = (
        lax.all_gather(w_query, "wshard", axis=0, tiled=True),
        lax.all_gather(w_key, "wshard", axis=0, tiled=True),
        lax.all_gather(w_value, "wshard", axis=0, tiled=True),
        lax.all_gather(w_out, "wshard", axis=0, tiled=True),
        lax.all_gather(w_gate, "wshard", axis=0, tiled=True),
        lax.all_gather(w_up, "wshard", axis=0, tiled=True),
        lax.all_gather(w_down, "wshard", axis=0, tiled=True),
        lax.all_gather(gain_in, "wshard", axis=0, tiled=True),
        lax.all_gather(gain_attn_post, "wshard", axis=0, tiled=True),
        lax.all_gather(gain_ff_pre, "wshard", axis=0, tiled=True),
        lax.all_gather(gain_ff_post, "wshard", axis=0, tiled=True),
        lax.all_gather(gain_query, "wshard", axis=0, tiled=True),
        lax.all_gather(gain_key, "wshard", axis=0, tiled=True),
    )
    full_query, full_key, full_value, full_out, full_gate, full_up, full_down = gathered[:7]
    in_gain, attn_post_gain, ff_pre_gain, ff_post_gain, query_gain, key_gain = [
        g.astype(jnp.float32) for g in gathered[7:]
    ]
    row_count = inputs.shape[0]
    head_dim = full_key.shape[1]
    head_count = full_query.shape[1] // head_dim
    score_scale = head_dim ** (-0.5)
    start_row = lax.axis_index(("seq", "wshard")) * row_count
    query_pos = start_row + jnp.arange(row_count, dtype=jnp.int32)
    cos_table, sin_table = rope_tables(query_pos, head_dim)
    x_float = inputs.astype(jnp.float32)
    normed_in = rms_gain(x_float, in_gain).astype(jnp.bfloat16)
    query_raw = jnp.dot(normed_in, full_query, preferred_element_type=jnp.float32).reshape(
        row_count, head_count, head_dim
    )
    key_raw = jnp.dot(normed_in, full_key, preferred_element_type=jnp.float32)[:, None, :]
    values = jnp.dot(normed_in, full_value, preferred_element_type=jnp.float32).astype(jnp.bfloat16)
    queries = norm_rope(query_raw, query_gain, cos_table, sin_table).astype(jnp.bfloat16)
    key_rot = norm_rope(key_raw, key_gain, cos_table, sin_table)[:, 0].astype(jnp.bfloat16)
    sent_rows = min(WINDOW, row_count)
    hop_count = WINDOW // sent_rows
    outgoing = (key_rot, values, doc_ids)
    halo_keys = []
    halo_values = []
    halo_docs = []
    for distance in range(hop_count, 0, -1):
        arrived = from_behind((outgoing[0], outgoing[1], outgoing[2]), ("seq", "wshard"), distance)
        halo_keys.append(arrived[0])
        halo_values.append(arrived[1])
        halo_docs.append(arrived[2])
    all_keys = jnp.concatenate(halo_keys + [key_rot], 0)
    all_values = jnp.concatenate(halo_values + [values], 0)
    all_docs = jnp.concatenate(halo_docs + [doc_ids], 0)
    key_pos = start_row - WINDOW + jnp.arange(WINDOW + row_count, dtype=jnp.int32)
    allowed = window_mask(query_pos, key_pos, doc_ids, all_docs)
    scores = masked_scores(queries, all_keys, allowed, score_scale)
    row_peak = jnp.max(scores, axis=-1, keepdims=True)
    row_total = jnp.sum(
        jnp.where(allowed[None], jnp.exp(scores - row_peak), 0.0), axis=-1, keepdims=True
    )
    log_total = row_peak + jnp.log(row_total)
    soft = jnp.where(allowed[None], jnp.exp(scores - log_total), 0.0).astype(jnp.bfloat16)
    attended = jnp.einsum("hqk,kd->qhd", soft, all_values, preferred_element_type=jnp.float32)
    attended = attended.reshape(row_count, head_count * head_dim).astype(jnp.bfloat16)
    attn_proj = jnp.dot(attended, full_out, preferred_element_type=jnp.float32)
    resid = x_float + rms_gain(attn_proj, attn_post_gain)
    normed_ff = rms_gain(resid, ff_pre_gain).astype(jnp.bfloat16)
    gate_pre = jnp.dot(normed_ff, full_gate, preferred_element_type=jnp.float32)
    up_pre = jnp.dot(normed_ff, full_up, preferred_element_type=jnp.float32)
    hidden = geglu(gate_pre, up_pre).astype(jnp.bfloat16)
    ff_proj = jnp.dot(hidden, full_down, preferred_element_type=jnp.float32)
    layer_out = (resid + rms_gain(ff_proj, ff_post_gain)).astype(jnp.bfloat16)
    grad_top = cotangent.astype(jnp.float32)
    _, pullback = jax.vjp(rms_gain, ff_proj, ff_post_gain)
    grad_ff_proj, grad_gain_ff_post = pullback(grad_top)
    grad_ff_proj = grad_ff_proj.astype(jnp.bfloat16)
    grad_w_down = weight_grad(hidden, grad_ff_proj)
    grad_hidden = lax.dot_general(
        grad_ff_proj, full_down, (((1,), (1,)), ((), ())), preferred_element_type=jnp.float32
    )
    _, pullback = jax.vjp(geglu, gate_pre, up_pre)
    grad_gate, grad_up = pullback(grad_hidden)
    grad_gate = grad_gate.astype(jnp.bfloat16)
    grad_up = grad_up.astype(jnp.bfloat16)
    grad_w_gate = weight_grad(normed_ff, grad_gate)
    grad_w_up = weight_grad(normed_ff, grad_up)
    grad_normed_ff = lax.dot_general(
        grad_gate, full_gate, (((1,), (1,)), ((), ())), preferred_element_type=jnp.float32
    )
    grad_normed_ff = grad_normed_ff + lax.dot_general(
        grad_up, full_up, (((1,), (1,)), ((), ())), preferred_element_type=jnp.float32
    )
    _, pullback = jax.vjp(rms_gain, resid, ff_pre_gain)
    grad_resid_part, grad_gain_ff_pre = pullback(grad_normed_ff)
    grad_resid = grad_top + grad_resid_part
    ff_gradients = (grad_w_gate, grad_w_up, grad_w_down, grad_gain_ff_pre, grad_gain_ff_post)
    ff_parts = (
        lax.psum_scatter(
            ff_gradients[0].astype(jnp.bfloat16), "wshard", scatter_dimension=0, tiled=True
        ).astype(jnp.float32),
        lax.psum_scatter(
            ff_gradients[1].astype(jnp.bfloat16), "wshard", scatter_dimension=0, tiled=True
        ).astype(jnp.float32),
        lax.psum_scatter(
            ff_gradients[2].astype(jnp.bfloat16), "wshard", scatter_dimension=0, tiled=True
        ).astype(jnp.float32),
        lax.psum_scatter(
            ff_gradients[3].astype(jnp.bfloat16), "wshard", scatter_dimension=0, tiled=True
        ).astype(jnp.float32),
        lax.psum_scatter(
            ff_gradients[4].astype(jnp.bfloat16), "wshard", scatter_dimension=0, tiled=True
        ).astype(jnp.float32),
    )
    ff_reduced = (
        lax.psum(ff_parts[0].astype(jnp.bfloat16), "seq").astype(jnp.float32),
        lax.psum(ff_parts[1].astype(jnp.bfloat16), "seq").astype(jnp.float32),
        lax.psum(ff_parts[2].astype(jnp.bfloat16), "seq").astype(jnp.float32),
        lax.psum(ff_parts[3].astype(jnp.bfloat16), "seq").astype(jnp.float32),
        lax.psum(ff_parts[4].astype(jnp.bfloat16), "seq").astype(jnp.float32),
    )
    _, pullback = jax.vjp(rms_gain, attn_proj, attn_post_gain)
    grad_attn_proj, grad_gain_attn_post = pullback(grad_resid)
    grad_attn_proj = grad_attn_proj.astype(jnp.bfloat16)
    grad_w_out = weight_grad(attended, grad_attn_proj)
    grad_attended = lax.dot_general(
        grad_attn_proj, full_out, (((1,), (1,)), ((), ())), preferred_element_type=jnp.float32
    ).astype(jnp.bfloat16)
    grad_heads = grad_attended.reshape(row_count, head_count, head_dim)
    again_scores = masked_scores(queries, all_keys, allowed, score_scale)
    probs = jnp.where(allowed[None], jnp.exp(again_scores - log_total), 0.0)
    grad_soft = jnp.einsum(
        "qhd,kd->hqk", grad_heads, all_values, preferred_element_type=jnp.float32
    )
    row_inner = jnp.sum(probs * grad_soft, axis=-1, keepdims=True)
    grad_score = (probs * (grad_soft - row_inner) * score_scale).astype(jnp.bfloat16)
    grad_queries = jnp.einsum(
        "hqk,kd->qhd", grad_score, all_keys, preferred_element_type=jnp.float32
    )
    grad_keys_all = jnp.einsum(
        "hqk,qhd->kd", grad_score, queries, preferred_element_type=jnp.float32
    )
    grad_values_all = jnp.einsum(
        "hqk,qhd->kd", probs.astype(jnp.bfloat16), grad_heads, preferred_element_type=jnp.float32
    )
    back_keys = jnp.zeros((sent_rows, head_dim), jnp.float32)
    back_values = jnp.zeros((sent_rows, head_dim), jnp.float32)
    for piece_index in range(hop_count):
        distance = hop_count - piece_index
        piece_start = piece_index * sent_rows
        arrived = (
            from_behind(
                grad_keys_all[piece_start : piece_start + sent_rows].astype(jnp.bfloat16),
                ("seq", "wshard"),
                -distance,
            ).astype(jnp.float32),
            from_behind(
                grad_values_all[piece_start : piece_start + sent_rows].astype(jnp.bfloat16),
                ("seq", "wshard"),
                -distance,
            ).astype(jnp.float32),
        )
        back_keys = back_keys + arrived[0]
        back_values = back_values + arrived[1]
    own_keys = grad_keys_all[WINDOW:]
    own_values = grad_values_all[WINDOW:]
    split_row = row_count - sent_rows
    grad_keys = jnp.concatenate([own_keys[:split_row], own_keys + back_keys], 0)
    grad_values = jnp.concatenate([own_values[:split_row], own_values + back_values], 0).astype(
        jnp.bfloat16
    )

    def query_path(tensor, gain_vec):
        return norm_rope(tensor, gain_vec, cos_table, sin_table)

    _, pullback = jax.vjp(query_path, query_raw, query_gain)
    grad_query_raw, grad_gain_query = pullback(grad_queries)
    _, pullback = jax.vjp(query_path, key_raw, key_gain)
    grad_key_raw, grad_gain_key = pullback(grad_keys[:, None, :])
    grad_query_raw = grad_query_raw.reshape(row_count, head_count * head_dim).astype(jnp.bfloat16)
    grad_key_raw = grad_key_raw[:, 0].astype(jnp.bfloat16)
    grad_w_query = weight_grad(normed_in, grad_query_raw)
    grad_w_key = weight_grad(normed_in, grad_key_raw)
    grad_w_value = weight_grad(normed_in, grad_values)
    grad_normed_in = lax.dot_general(
        grad_query_raw, full_query, (((1,), (1,)), ((), ())), preferred_element_type=jnp.float32
    )
    grad_normed_in = grad_normed_in + lax.dot_general(
        grad_key_raw, full_key, (((1,), (1,)), ((), ())), preferred_element_type=jnp.float32
    )
    grad_normed_in = grad_normed_in + lax.dot_general(
        grad_values, full_value, (((1,), (1,)), ((), ())), preferred_element_type=jnp.float32
    )
    _, pullback = jax.vjp(rms_gain, x_float, in_gain)
    grad_input_part, grad_gain_in = pullback(grad_normed_in)
    grad_inputs = grad_resid + grad_input_part
    attn_gradients = (
        grad_w_query,
        grad_w_key,
        grad_w_value,
        grad_w_out,
        grad_gain_in,
        grad_gain_attn_post,
        grad_gain_query,
        grad_gain_key,
    )
    attn_parts = (
        lax.psum_scatter(
            attn_gradients[0].astype(jnp.bfloat16), "wshard", scatter_dimension=0, tiled=True
        ).astype(jnp.float32),
        lax.psum_scatter(
            attn_gradients[1].astype(jnp.bfloat16), "wshard", scatter_dimension=0, tiled=True
        ).astype(jnp.float32),
        lax.psum_scatter(
            attn_gradients[2].astype(jnp.bfloat16), "wshard", scatter_dimension=0, tiled=True
        ).astype(jnp.float32),
        lax.psum_scatter(
            attn_gradients[3].astype(jnp.bfloat16), "wshard", scatter_dimension=0, tiled=True
        ).astype(jnp.float32),
        lax.psum_scatter(
            attn_gradients[4].astype(jnp.bfloat16), "wshard", scatter_dimension=0, tiled=True
        ).astype(jnp.float32),
        lax.psum_scatter(
            attn_gradients[5].astype(jnp.bfloat16), "wshard", scatter_dimension=0, tiled=True
        ).astype(jnp.float32),
        lax.psum_scatter(
            attn_gradients[6].astype(jnp.bfloat16), "wshard", scatter_dimension=0, tiled=True
        ).astype(jnp.float32),
        lax.psum_scatter(
            attn_gradients[7].astype(jnp.bfloat16), "wshard", scatter_dimension=0, tiled=True
        ).astype(jnp.float32),
    )
    attn_reduced = (
        lax.psum(attn_parts[0].astype(jnp.bfloat16), "seq").astype(jnp.float32),
        lax.psum(attn_parts[1].astype(jnp.bfloat16), "seq").astype(jnp.float32),
        lax.psum(attn_parts[2].astype(jnp.bfloat16), "seq").astype(jnp.float32),
        lax.psum(attn_parts[3].astype(jnp.bfloat16), "seq").astype(jnp.float32),
        lax.psum(attn_parts[4].astype(jnp.bfloat16), "seq").astype(jnp.float32),
        lax.psum(attn_parts[5].astype(jnp.bfloat16), "seq").astype(jnp.float32),
        lax.psum(attn_parts[6].astype(jnp.bfloat16), "seq").astype(jnp.float32),
        lax.psum(attn_parts[7].astype(jnp.bfloat16), "seq").astype(jnp.float32),
    )
    reduced = (
        attn_reduced[0],
        attn_reduced[1],
        attn_reduced[2],
        attn_reduced[3],
        ff_reduced[0],
        ff_reduced[1],
        ff_reduced[2],
        attn_reduced[4],
        attn_reduced[5],
        ff_reduced[3],
        ff_reduced[4],
        attn_reduced[6],
        attn_reduced[7],
    )
    return (layer_out, grad_inputs) + tuple(reduced)


def solution(mesh):
    routed = mesh.shape["wshard"] == 2 and mesh.shape["seq"] == 16
    return jax.shard_map(
        per_device if routed else per_device_general,
        mesh=mesh,
        in_specs=(
            P(("seq", "wshard"), None),
            P(("seq", "wshard")),
            P("wshard", None),
            P("wshard", None),
            P("wshard", None),
            P("wshard", None),
            P("wshard", None),
            P("wshard", None),
            P("wshard", None),
            P("wshard"),
            P("wshard"),
            P("wshard"),
            P("wshard"),
            P("wshard"),
            P("wshard"),
            P(("seq", "wshard"), None),
        ),
        out_specs=(
            P(("seq", "wshard"), None),
            P(("seq", "wshard"), None),
            P("wshard", None),
            P("wshard", None),
            P("wshard", None),
            P("wshard", None),
            P("wshard", None),
            P("wshard", None),
            P("wshard", None),
            P("wshard"),
            P("wshard"),
            P("wshard"),
            P("wshard"),
            P("wshard"),
            P("wshard"),
        ),
        check_vma=False,
    )
```

profile of v0, /device:TPU:0, one launch (start us, length us, event | category | flops | bytes accessed | tf_op | source)
XLA Modules:
  0.0 271.5 jit_solution(8852543411733701327)
XLA Ops:
  0.7 4.2 %concatenate.27 = bf16[1536]{0:T(1024)(128)(2,1)S(1)} concatenate(bf16[320]{0:T(512)(128)(2,1)} %param.25, bf16[320]{0:T(512)(128)(2,1)} %param.26, bf16[320]{0:T(512)(128)(2,1)} %param.27, bf16[320]{0:T(512)(128)(2,1)} %param.28, bf16[128]{0:T(256)(128)(2,1)} %param.29, bf16[128]{0:T(256)(128)(2,1)} %param.30), dimensions={0} | concatenate | bytes 6144 | tf_op jit(solution)/shard_map/concatenate | solution.py:579
  5.5 49.7 %gather_weights.1 = (bf16[640,1024]{1,0:T(8,128)(2,1)}, bf16[640,256]{1,0:T(8,128)(2,1)}, bf16[640,256]{1,0:T(8,128)(2,1)}, bf16[1024,640]{1,0:T(8,128)(2,1)}, b...) custom-call(bf16[320,1024]{1,0:T(8,128)(2,1)} %refs_0_.1, ...), custom_call_target="tpu_custom_call" | custom-call | tf_op jit(solution)/shard_map/gather_weights/pallas_call | solution.py:168
  55.2 0.8 copy.140
  56.6 2.0 convolution_convert_fusion.2.refs_1_
  58.7 1.3 multiply_reduce_fusion.9
  60.8 0.7 maximum_bitcast_fusion.6.refs_0_
  61.5 9.5 %shift_on.1 = (bf16[2,256,256]{2,1,0:T(8,128)(2,1)}, bf16[2,256,256]{2,1,0:T(8,128)(2,1)}, s32[2,2,128]{2,1,0:T(2,128)}) custom-call(bf16[256,256]{1,0:T(8,128)(2,1)} %maximum_bitcast_fusion.6.refs_0_, bf16[256,256]{1,0:T(8,128)(2,1)} %convolution_convert_fusion.2.refs_1_, s32[2,128]{1,0:T(2,128)} %bitcast.196), custom_call_target="tpu_custom_call" | custom-call | tf_op jit(solution)/shard_map/shift_on/pallas_call | solution.py:544
  71.0 1.7 slice_bitcast_fusion.3
  72.8 0.7 slice_bitcast_fusion.6
  73.5 0.9 fusion.25
  77.7 0.7 fusion.4
  78.5 0.8 select_reduce_fusion
  79.9 1.0 convolution_convert_fusion.1
  81.2 0.7 multiply_reduce_fusion.8
  82.5 2.9 %fusion.87 = f32[256,2048]{1,0:T(8,128)S(1)} fusion(bf16[256,640]{1,0:T(8,128)(2,1)S(1)} %multiply_convert_fusion.2.refs_0_.refs_1_, bf16[640,2048]{1,0:T(8,128)(2,1)} %get-tuple-element.45), kind=kOutput, calls=%fused_computation.192 | convolution fusion | flops 671088640 | bytes 5046272 | tf_op jit(solution)/shard_map/dot_general | solution.py:633
  85.4 2.6 multiply_convert_fusion.1
  88.0 1.0 copy-done.33
  89.0 1.8 multiply_reduce_fusion.6
  90.9 1.5 fusion.33
  92.4 2.1 fusion.34
  94.5 4.6 %multiply_convert_fusion = (bf16[256,2048]{1,0:T(8,128)(2,1)S(1)}, bf16[256,2048]{1,0:T(8,128)(2,1)S(1)}) fusion(f32[256,2048]{1,0:T(8,128)S(1)} %copy-done.20, f32[256,2048]{1,0:T(8,128)} %get-tuple-element.113, bf16[256,640]{1,0:T(8,128)(2,1)S(1)} %get-tuple-element.80.refs_8_, bf16[2048,640]{1,0:T(8,128)(2,1)} %get-tuple-element.47), kind=kOutput, calls=%fused_computation.19 | convolution fusion | flops 683671552 | bytes 9240576 | tf_op jit(solution)/shard_map/dot_general | solution.py:642
  99.1 1.0 fusion.88
  100.2 1.4 copy-done.16
  101.6 1.4 multiply_reduce_fusion.2
  105.0 2.3 fusion.40
  107.3 7.8 %fusion.16 = f32[768,256]{1,0:T(8,128)} fusion(f32[768,256,4]{1,0,2:T(8,128)} %fusion.40, bf16[256,4,128]{2,0,1:T(8,128)(2,1)} %copy-done.44, bf16[256,4,128]{2,0,1:T(8,128)(2,1)} %copy-done.43, f32[768,256,4]{1,0,2:T(8,128)} %copy-done.11, f32[4,256]{1,0:T(4,128)S(1)} %copy-done.50, pred[256,768]{0,1:T(8,128)(4,1)S(1)} %copy-done.36), kind=kOutput, calls=%fused_computation.32 | convolution fusion | flops 413927168 | bytes 7802880 | tf_op jit(solution)/shard_map/hqk,qhd->kd/dot_general | solution.py:675
  115.1 1.8 slice.134
  116.9 2.8 %convolution_bitcast_fusion = f32[768,256]{1,0:T(8,128)S(1)} fusion(bf16[32,4,8,256]{3,2,1,0:T(8,128)(2,1)S(1)} %bitcast.190, f32[768,256,4]{1,0,2:T(8,128)} %copy-done.11, f32[4,256]{1,0:T(4,128)S(1)} %copy-done.50, pred[256,768]{0,1:T(8,128)(4,1)S(1)} %copy-done.36), kind=kOutput, calls=%fused_computation.34 | convolution fusion | flops 406585344 | bytes 4657152 | tf_op jit(solution)/shard_map/hqk,qhd->kd/dot_general | solution.py:678
  119.8 0.9 copy-done.42
  120.6 0.7 slice.133
  121.4 11.9 %shift_back.1 = (bf16[2,256,256]{2,1,0:T(8,128)(2,1)}, bf16[2,256,256]{2,1,0:T(8,128)(2,1)}) custom-call(bf16[2,256,256]{2,1,0:T(8,128)(2,1)} %bitcast.191, bf16[2,256,256]{2,1,0:T(8,128)(2,1)} %bitcast.192), custom_call_target="tpu_custom_call" | custom-call | tf_op jit(solution)/shard_map/shift_back/pallas_call | solution.py:544
  133.3 1.0 convert_reduce_fusion
  134.3 1.0 fusion.47
  135.3 1.3 fusion.90
  136.7 1.0 convert_reduce_fusion.1
  137.7 1.0 fusion.48
  139.6 0.6 copy-done.29
  140.3 1.1 fusion.89
  141.4 8.3 %fusion.15 = f32[256,4,256]{2,0,1:T(8,128)} fusion(f32[768,256,4]{1,0,2:T(8,128)} %fusion.40, bf16[256,256]{1,0:T(8,128)(2,1)} %maximum_bitcast_fusion.6.refs_0_, bf16[256,256]{1,0:T(8,128)(2,1)} %copy-done.47, bf16[256,256]{1,0:T(8,128)(2,1)} %copy-done.46, f32[768,256,4]{1,0,2:T(8,128)} %copy-done.11, f32[4,256]{1,0:T(4,128)S(1)} %copy-done.50, ...), kind=kOutput, calls=%fused_computation.26 | convolution fusion | flops 414058240 | bytes 7933952 | tf_op jit(solution)/shard_map/hqk,kd->qhd/dot_general | solution.py:672
  149.7 1.3 multiply_add_fusion.1
  152.5 0.8 fusion.31
  153.4 1.1 fusion.36
  154.4 1.0 copy.119.refs_5_
  155.4 0.7 pad_maximum_fusion.3.refs_10_
  157.9 98.1 %reduce_terms.1 = (bf16[17,2,2,4,80,128]{5,4,3,2,1,0:T(8,128)(2,1)}, f32[4,24,128]{2,1,0:T(8,128)}) custom-call(bf16[256,640]{1,0:T(8,128)(2,1)} %copy-done.2, bf16[256,640]{1,0:T(8,128)(2,1)} %copy-done.2, bf16[256,2048]{1,0:T(8,128)(2,1)} %copy-done.33, bf16[256,640]{1,0:T(8,128)(2,1)} %copy-done, bf16[256,640]{1,0:T(8,128)(2,1)} %copy-done, ...), custom_call_target="tpu_custom_call" | custom-call | tf_op jit(solution)/shard_map/reduce_terms/pallas_call | solution.py:402
  256.1 13.5 %unpack.1 = (f32[320,2048]{1,0:T(8,128)}, f32[320,2048]{1,0:T(8,128)}, f32[1024,640]{1,0:T(8,128)}, f32[320,1024]{1,0:T(8,128)}, f32[320,256]{1,0:T(8,128)}, /*index=5*/f32[320,256]{1,0:T(8,128)}, f32[512,640]{1,0:T(8,128)}) custom-call(bf16[17,2,2,4,80,128]{5,4,3,2,1,0:T(8,128)(2,1)} %get-tuple-element.50.summed), custom_call_target="tpu_custom_call" | custom-call | tf_op jit(solution)/shard_map/unpack/pallas_call | solution.py:479
  269.5 0.7 slice_bitcast_fusion.4
  270.2 0.7 fusion.85
  (158 shorter events, 13.4 us)
Async XLA Ops:
  0.6 55.7 %copy-start.1 = (bf16[256,640]{1,0:T(8,128)(2,1)S(1)}, bf16[256,640]{1,0:T(8,128)(2,1)}, u32[]{:S(2)}) copy-start(bf16[256,640]{1,0:T(8,128)(2,1)} %param.16) | copy-start | bytes 983044
  55.2 18.2 %copy-start.48 = (s32[256]{0:T(256)S(1)}, s32[256]{0:T(256)}, u32[]{:S(2)}) copy-start(s32[256]{0:T(256)} %param.17) | copy-start | bytes 3076
  55.2 19.2 %copy-start.3 = (bf16[640,1024]{1,0:T(8,128)(2,1)S(1)}, bf16[640,1024]{1,0:T(8,128)(2,1)}, u32[]{:S(2)}) copy-start(bf16[640,1024]{1,0:T(8,128)(2,1)} %get-tuple-element.43) | copy-start | bytes 3932164
  56.6 18.4 %copy-start = (bf16[256,640]{1,0:T(8,128)(2,1)}, bf16[256,640]{1,0:T(8,128)(2,1)S(1)}, u32[]{:S(2)}) copy-start(bf16[256,640]{1,0:T(8,128)(2,1)S(1)} %fusion.30.refs_3_.refs_4_) | copy-start | bytes 983044
  60.1 14.3 %copy-start.8 = (f32[256,256]{1,0:T(8,128)}, f32[256,256]{1,0:T(8,128)S(1)}, u32[]{:S(2)}) copy-start(f32[256,256]{1,0:T(8,128)S(1)} %copy.97) | copy-start | bytes 786436
  74.4 4.9 %copy-start.35 = (pred[256,768]{0,1:T(8,128)(4,1)}, pred[256,768]{0,1:T(8,128)(4,1)S(1)}, u32[]{:S(2)}) copy-start(pred[256,768]{0,1:T(8,128)(4,1)S(1)} %fusion.25) | copy-start | bytes 589828
  75.5 1.4 copy-start.45
  75.5 2.2 copy-start.37
  76.7 1.6 copy-start.25
  76.9 1.5 copy-start.43
  77.0 2.3 copy-start.46
  78.4 2.5 copy-start.11
  78.4 1.0 copy-start.31
  78.4 1.3 copy-start.38
  78.4 1.5 copy-start.40
  79.9 1.1 copy-start.49
  79.9 1.3 copy-start.5
  81.0 1.3 copy-start.21
  82.3 3.1 %copy-start.15 = (bf16[640,2048]{1,0:T(8,128)(2,1)S(1)}, bf16[640,2048]{1,0:T(8,128)(2,1)}, u32[]{:S(2)}) copy-start(bf16[640,2048]{1,0:T(8,128)(2,1)} %get-tuple-element.46) | copy-start | bytes 7864324
  82.5 5.5 %copy-start.2 = (bf16[256,640]{1,0:T(8,128)(2,1)}, bf16[256,640]{1,0:T(8,128)(2,1)S(1)}, u32[]{:S(2)}) copy-start(bf16[256,640]{1,0:T(8,128)(2,1)S(1)} %multiply_convert_fusion.2.refs_0_.refs_1_) | copy-start | bytes 983044
  85.4 2.6 copy-start.19
  85.4 3.6 %copy-start.51 = (bf16[2048,640]{1,0:T(8,128)(2,1)S(1)}, bf16[2048,640]{1,0:T(8,128)(2,1)}, u32[]{:S(2)}) copy-start(bf16[2048,640]{1,0:T(8,128)(2,1)} %get-tuple-element.47) | copy-start | bytes 7864324
  88.0 1.0 copy-start.33
  88.0 2.9 %copy-start.13 = (bf16[256,640]{1,0:T(8,128)(2,1)S(1)}, bf16[256,640]{1,0:T(8,128)(2,1)}, u32[]{:S(2)}) copy-start(bf16[256,640]{1,0:T(8,128)(2,1)} %param.31) | copy-start | bytes 983044
  90.9 3.6 %copy-start.20 = (f32[256,2048]{1,0:T(8,128)S(1)}, f32[256,2048]{1,0:T(8,128)}, u32[]{:S(2)}) copy-start(f32[256,2048]{1,0:T(8,128)} %copy-done.19) | copy-start | bytes 6291460
  94.5 4.6 %copy-start.23 = (bf16[256,640]{1,0:T(8,128)(2,1)}, bf16[256,640]{1,0:T(8,128)(2,1)S(1)}, u32[]{:S(2)}) copy-start(bf16[256,640]{1,0:T(8,128)(2,1)S(1)} %get-tuple-element.80.refs_8_) | copy-start | bytes 983044
  94.5 4.6 %copy-start.17 = (bf16[640,2048]{1,0:T(8,128)(2,1)S(1)}, bf16[640,2048]{1,0:T(8,128)(2,1)}, u32[]{:S(2)}) copy-start(bf16[640,2048]{1,0:T(8,128)(2,1)} %get-tuple-element.45) | copy-start | bytes 7864324
  99.1 4.0 %copy-start.10 = (bf16[256,2048]{1,0:T(8,128)(2,1)}, bf16[256,2048]{1,0:T(8,128)(2,1)S(1)}, u32[]{:S(2)}) copy-start(bf16[256,2048]{1,0:T(8,128)(2,1)S(1)} %get-tuple-element.74.refs_7_) | copy-start | bytes 3145732
  99.1 4.0 %copy-start.34 = (bf16[256,2048]{1,0:T(8,128)(2,1)}, bf16[256,2048]{1,0:T(8,128)(2,1)S(1)}, u32[]{:S(2)}) copy-start(bf16[256,2048]{1,0:T(8,128)(2,1)S(1)} %get-tuple-element.75.refs_6_) | copy-start | bytes 3145732
  99.1 2.5 copy-start.16
  100.1 2.9 %copy-start.14 = (bf16[256,640]{1,0:T(8,128)(2,1)S(1)}, bf16[256,640]{1,0:T(8,128)(2,1)}, u32[]{:S(2)}) copy-start(bf16[256,640]{1,0:T(8,128)(2,1)} %param.31) | copy-start | bytes 983044
  103.1 1.3 copy-start.6
  103.1 1.9 copy-start.32
  103.1 1.9 copy-start.39
  103.1 1.9 copy-start.41
  104.4 10.8 %copy-start.12 = (bf16[256,640]{1,0:T(8,128)(2,1)}, bf16[256,640]{1,0:T(8,128)(2,1)S(1)}, u32[]{:S(2)}) copy-start(bf16[256,640]{1,0:T(8,128)(2,1)S(1)} %fusion.35.refs_11_) | copy-start | bytes 983044
  104.4 2.9 %copy-start.36 = (pred[256,768]{0,1:T(8,128)(4,1)S(1)}, pred[256,768]{0,1:T(8,128)(4,1)}, u32[]{:S(2)}) copy-start(pred[256,768]{0,1:T(8,128)(4,1)} %copy-done.35) | copy-start | bytes 589828
  104.4 2.9 %copy-start.50 = (f32[4,256]{1,0:T(4,128)S(1)}, f32[4,256]{1,0:T(4,128)}, u32[]{:S(2)}) copy-start(f32[4,256]{1,0:T(4,128)} %copy-done.49) | copy-start | bytes 12292
  120.6 18.6 %copy-start.9 = (f32[256,256]{1,0:T(8,128)S(1)}, f32[256,256]{1,0:T(8,128)}, u32[]{:S(2)}) copy-start(f32[256,256]{1,0:T(8,128)} %copy-done.8) | copy-start | bytes 786436
  120.6 19.6 %copy-start.24 = (bf16[640,256]{1,0:T(8,128)(2,1)S(1)}, bf16[640,256]{1,0:T(8,128)(2,1)}, u32[]{:S(2)}) copy-start(bf16[640,256]{1,0:T(8,128)(2,1)} %get-tuple-element.38) | copy-start | bytes 983044
  135.3 2.3 copy-start.27
  141.4 8.3 %copy-start.26 = (f32[256,128]{1,0:T(8,128)S(1)}, f32[256,128]{1,0:T(8,128)}, u32[]{:S(2)}) copy-start(f32[256,128]{1,0:T(8,128)} %copy-done.25) | copy-start | bytes 393220
  151.0 1.3 copy-start.4
  151.1 1.5 copy-start.18
  152.0 2.4 copy-start.7
  152.5 1.9 copy-start.22
  152.5 2.9 %copy-start.28 = (bf16[256,256]{1,0:T(8,128)(2,1)S(1)}, bf16[256,256]{1,0:T(8,128)(2,1)}, u32[]{:S(2)}) copy-start(bf16[256,256]{1,0:T(8,128)(2,1)} %copy-done.27) | copy-start | bytes 393220
  152.5 2.9 %copy-start.30 = (bf16[256,256]{1,0:T(8,128)(2,1)S(1)}, bf16[256,256]{1,0:T(8,128)(2,1)}, u32[]{:S(2)}) copy-start(bf16[256,256]{1,0:T(8,128)(2,1)} %copy-done.29) | copy-start | bytes 393220
  (4 other events, 3.0 us)
where the time goes:
time: 273 us; the launch traced here: 271 us
  Pallas kernels  183 us (67%)
  matrix products  45.7 us (17%)
  local copies, waits for them, and re-layouts  22 us (8%)
  other arithmetic  19.5 us (7%)
    pallas_call x1, Pallas kernels, reduce_terms(): pl.pallas_call(functools.partial(reduce_kernel, len(lefts)), out_shape=[j...  98.1 us
    pallas_call x1, Pallas kernels, gather_weights(): pl.pallas_call(functools.partial(gather_kernel, count), out_shape=[jax.Sh...  49.7 us
    pallas_call x2, Pallas kernels, shift(): pl.pallas_call(functools.partial(shift_kernel, count, hops, step), out_sh...  21.5 us
    pallas_call x1, Pallas kernels, unpack(): pl.pallas_call(functools.partial(unpack_kernel, plan), grid=(chunks,), ou...  13.5 us
    unnamed x110, local copies, waits for them, and re-layouts  8.67 us
    dot_general x1, matrix products, per_device(): jnp.einsum('hqk,kd->qhd', grad_score, all_keys, preferred_element_type=jn...  8.3 us
    dot_general x1, matrix products, per_device(): jnp.einsum('hqk,qhd->kd', grad_score, queries, preferred_element_type=jnp...  7.8 us

commit v1 on v0

v1 whole, which is shorter than its diff:
```python
import functools
import types
import typing

import jax
import jax.numpy as jnp
from jax import lax
from jax.experimental import pallas as pl
from jax.experimental.pallas import tpu as pltpu
from jax.sharding import PartitionSpec as P

WINDOW = 512


NORM_EPSILON = 1e-06
ROPE_BASE = 10000.0
MASK_FLOOR = -1e30


def from_behind(array, axis, by):
    count = lax.axis_size(axis)
    pairs = [(i, i + by) for i in range(count) if 0 <= i + by < count]
    return lax.ppermute(array, axis, pairs)


def rms_gain(tensor, gain_vec):
    factor = lax.rsqrt(jnp.mean(tensor * tensor, axis=-1, keepdims=True) + NORM_EPSILON)
    return tensor * factor * (1.0 + gain_vec)


def rope_tables(positions, head_width):
    half_width = head_width // 2
    exponent = jnp.arange(half_width, dtype=jnp.float32) * (2.0 / head_width)
    inverse = jnp.exp(-jnp.log(ROPE_BASE) * exponent)
    angles = positions.astype(jnp.float32)[:, None] * inverse[None, :]
    return (jnp.cos(angles), jnp.sin(angles))


def norm_rope(tensor, gain_vec, cos_table, sin_table):
    normed = rms_gain(tensor, gain_vec)
    half_width = tensor.shape[-1] // 2
    front_part = normed[..., :half_width]
    back_part = normed[..., half_width:]
    cos_rows = cos_table[:, None, :]
    sin_rows = sin_table[:, None, :]
    return jnp.concatenate(
        [
            front_part * cos_rows - back_part * sin_rows,
            back_part * cos_rows + front_part * sin_rows,
        ],
        axis=-1,
    )


def geglu(gate_pre, up_pre):
    return jax.nn.gelu(gate_pre, approximate=True) * up_pre


def window_mask(query_pos, key_pos, query_doc, key_doc):
    distance = query_pos[:, None] - key_pos[None, :]
    return (
        (distance >= 0)
        & (distance < WINDOW)
        & (key_pos[None, :] >= 0)
        & (query_doc[:, None] == key_doc[None, :])
    )


def masked_scores(queries, all_keys, allowed, score_scale):
    scores = (
        jnp.einsum("qhd,kd->hqk", queries, all_keys, preferred_element_type=jnp.float32)
        * score_scale
    )
    return jnp.where(allowed[None], scores, MASK_FLOOR)


def weight_grad(left_rows, right_rows):
    return jnp.einsum("tc,tf->cf", left_rows, right_rows, preferred_element_type=jnp.float32)


MESH = pl.DeviceIdType.MESH
LANES = 128


def coordinates():
    seq = lax.axis_index("seq")
    return lax.rem(seq // 2, 2), lax.rem(seq, 2), seq // 4, lax.axis_index("wshard")


def device(x, core, z, y):
    return ((z * 2 + x) * 2 + core, y)


def greet(partners):
    barrier = pltpu.get_barrier_semaphore()
    for partner in partners:
        pl.semaphore_signal(barrier, inc=1, device_id=partner, device_id_type=MESH)
    pl.semaphore_wait(barrier, len(partners))


def remote(src, dst, send, recv, target):
    return pltpu.make_async_remote_copy(
        src_ref=src, dst_ref=dst, send_sem=send, recv_sem=recv,
        device_id=target, device_id_type=MESH,
    )


def token_dot(left, right):
    return lax.dot_general(
        left, right, (((0,), (0,)), ((), ())), preferred_element_type=jnp.float32
    ).astype(jnp.bfloat16)


GELU_SCALE = 0.7978845608028654
GELU_CUBE = 0.044715
GAIN_ROWS = 8
TERM_COLUMNS = 512


def dot(left, right):
    return jnp.dot(left, right, preferred_element_type=jnp.float32)


def dot_rows(left, right):
    return lax.dot_general(
        left, right, (((1,), (1,)), ((), ())), preferred_element_type=jnp.float32
    )


def dot_tokens(left, right):
    return lax.dot_general(
        left, right, (((0,), (0,)), ((), ())), preferred_element_type=jnp.float32
    )


def rms_factor(tensor):
    return lax.rsqrt(jnp.mean(tensor * tensor, axis=-1, keepdims=True) + NORM_EPSILON)


def rms_pull(tensor, gain_row, grad_out):
    factor = rms_factor(tensor)
    grad_normed = grad_out * (1.0 + gain_row)
    inner = jnp.mean(grad_normed * tensor, axis=-1, keepdims=True)
    grad_tensor = factor * grad_normed - tensor * (factor * factor * factor * inner)
    grad_gain = jnp.sum(grad_out * tensor * factor, axis=0, keepdims=True)
    return grad_tensor, grad_gain


def rotate(tensor, gain_row, cos_table, sin_table):
    half = tensor.shape[-1] // 2
    normed = tensor * rms_factor(tensor) * (1.0 + gain_row)
    front, back = normed[:, :half], normed[:, half:]
    return jnp.concatenate(
        [front * cos_table - back * sin_table, back * cos_table + front * sin_table], axis=-1
    )


def rotate_pull(tensor, gain_row, cos_table, sin_table, grad_out):
    half = tensor.shape[-1] // 2
    front, back = grad_out[:, :half], grad_out[:, half:]
    grad_normed = jnp.concatenate(
        [front * cos_table + back * sin_table, back * cos_table - front * sin_table], axis=-1
    )
    return rms_pull(tensor, gain_row, grad_normed)


def add_bf16(a, b):
    return (a.astype(jnp.float32) + b.astype(jnp.float32)).astype(jnp.bfloat16)


def lane_block(at, width):
    return pl.ds(pl.multiple_of(at * width, width), width)


class Weights(typing.NamedTuple):
    key: typing.Any
    value: typing.Any
    query: typing.Any
    out: typing.Any
    gate: typing.Any
    up: typing.Any
    down: typing.Any


class Inputs(typing.NamedTuple):
    x: typing.Any
    cotangent: typing.Any
    docs: typing.Any
    cos: typing.Any
    sin: typing.Any
    gains_own: typing.Any


class Outputs(typing.NamedTuple):
    layer_out: typing.Any
    grad_inputs: typing.Any
    summed: typing.Any
    gain_sums: typing.Any


class Sems(typing.NamedTuple):
    send: typing.Any
    recv: typing.Any


def layer_kernel(names, *refs):
    counts = [len(Inputs._fields), len(Weights._fields), len(Outputs._fields)]
    a, b, c = counts[0], counts[0] + counts[1], sum(counts)
    r = types.SimpleNamespace(**dict(zip(names, refs[c + counts[1] :])))
    for ref, name in zip(refs[:a] + refs[b:c], Inputs._fields + Outputs._fields):
        setattr(r, name, ref)
    shards, full = refs[a:b], Weights(*refs[c : c + counts[1]])
    x_ref, cot_ref, docs = r.x, r.cotangent, r.docs
    rows, dim = x_ref.shape
    head_dim = full.key.shape[1]
    heads = full.query.shape[1] // head_dim
    ff = full.gate.shape[1]
    score_scale = head_dim ** (-0.5)
    all_keys, all_values, halo_docs = r.all_keys, r.all_values, r.halo_docs
    hops = halo_docs.shape[0]
    span = hops * rows
    x, core, z, y = coordinates()
    depth = lax.axis_size("seq") // 4
    sibling = device(x, 1 - core, z, y)
    beside = device(1 - x, core, z, y)
    across = device(x, core, z, 1 - y)
    line = [device(x, core, lax.rem(z + d, depth), y) for d in range(1, depth)]
    width = lax.axis_size("wshard")
    total_devices = lax.axis_size("seq") * width
    me = lax.axis_index("seq") * width + lax.axis_index("wshard")

    def there(offset):
        return (me + offset >= 0) & (me + offset < total_devices)

    def neighbour(offset):
        place = lax.rem(me + offset + total_devices, total_devices)
        return (place // width, lax.rem(place, width))

    offsets = [d for d in range(-hops, hops + 1) if d != 0]
    greet([sibling, beside, across] + line + [neighbour(d) for d in offsets])

    half_ff = ff // 2
    items = [(0, None, 0, 1), (1, None, 0, 1), (2, None, 0, 1), (3, None, 0, 1)]
    for part in range(2):
        items += [(4, part, 0, 1), (5, part, 0, 1)]
    items += [(6, None, 0, 2), (6, None, 1, 2)]
    g_send, g_recv = r.g_send, r.g_recv

    def view(ref, low, high, part):
        if part is None:
            return ref.at[pl.ds(low, high)]
        return ref.at[pl.ds(low, high), pl.ds(part * half_ff, half_ff)]

    def geometry(i):
        name, part, piece, pieces = items[i]
        shard_rows = shards[name].shape[0]
        return name, part, shard_rows, shard_rows // 4, piece, shard_rows // 4 // pieces

    def first(i):
        name, part, shard_rows, quarter, piece, high = geometry(i)
        at = (core * 2 + x) * quarter + piece * high
        return remote(
            view(shards[name], at, high, part), view(full[name], y * shard_rows + at, high, part),
            g_send.at[0, i], g_recv.at[0, i], across,
        )

    def second(i):
        name, part, shard_rows, quarter, piece, high = geometry(i)
        at = (1 - y) * shard_rows + (core * 2 + x) * quarter + piece * high
        block = view(full[name], at, high, part)
        return remote(block, block, g_send.at[1, i], g_recv.at[1, i], beside)

    def third(i, side, slot):
        name, part, shard_rows, quarter, piece, high = geometry(i)
        at = (1 - y) * shard_rows + (core * 2 + side) * quarter + piece * high
        block = view(full[name], at, high, part)
        return remote(block, block, g_send.at[slot, i], g_recv.at[slot, i], sibling)

    def gain_gather():
        return remote(r.gains_own, r.gains_other, r.gain_gather_sems.at[0],
                      r.gain_gather_sems.at[1], across)

    def local(n):
        shard_rows = shards[n].shape[0]
        return pltpu.make_async_copy(
            shards[n], full[n].at[pl.ds(y * shard_rows, shard_rows)], r.own_sems.at[n]
        )

    def forward_one(i):
        first(i).wait_recv()
        second(i).start()
        third(i, x, 2).start()

    def forward_two(i):
        second(i).wait_recv()
        third(i, 1 - x, 3).start()

    def arrived(i):
        third(i, x, 2).wait_recv()
        third(i, 1 - x, 3).wait_recv()

    def shift_copy(k, d):
        slot = pl.ds((hops - d) * rows, rows)
        own = pl.ds(span, rows)
        if k == 0:
            src, dst = all_keys.at[own], all_keys.at[slot]
        elif k == 1:
            src, dst = all_values.at[own], all_values.at[slot]
        else:
            src, dst = docs, halo_docs.at[hops - d]
        return remote(src, dst, r.shift_send.at[k, d - 1], r.shift_recv.at[k, d - 1],
                      neighbour(d))

    def shift_start(kinds):
        for d in range(1, hops + 1):
            @pl.when(there(d))
            def _(d=d):
                for k in kinds:
                    shift_copy(k, d).start()

    def shift_arrive(kinds):
        for d in range(1, hops + 1):
            @pl.when(there(-d))
            def _(d=d):
                for k in kinds:
                    shift_copy(k, d).wait_recv()

            @pl.when(jnp.logical_not(there(-d)))
            def _(d=d):
                slot = slice((hops - d) * rows, (hops - d + 1) * rows)
                for k in kinds:
                    if k == 2:
                        halo_docs[hops - d] = jnp.zeros(docs.shape, docs.dtype)
                    else:
                        ref = (all_keys, all_values)[k]
                        ref[slot] = jnp.zeros((rows, head_dim), ref.dtype)

    gain_gather().start()
    for i in range(5):
        first(i).start()
    shift_start([2])
    for n in range(len(shards)):
        local(n).start()
    x_factor = rms_factor(x_ref[...].astype(jnp.float32))
    gain_gather().wait_recv()
    gains = r.gains
    gains[...] = r.gains_own[...] + r.gains_other[...]

    def gain(row, count=dim):
        return gains[row : row + 1, :count]

    normed_in = r.normed_in
    normed_in[...] = (
        x_ref[...].astype(jnp.float32) * x_factor * (1.0 + gain(0))
    ).astype(jnp.bfloat16)
    forward_one(0)
    forward_one(1)
    shift_arrive([2])
    bias = r.bias
    lane_tiles = docs.shape[0]
    query_docs = [
        jnp.transpose(jnp.broadcast_to(docs[k : k + 1].astype(jnp.float32), (LANES, LANES)))
        for k in range(lane_tiles)
    ]
    for block in range(lane_tiles * (hops + 1)):
        hop, k = block // lane_tiles, block % lane_tiles
        source = docs[k : k + 1] if hop == hops else halo_docs[hop, k : k + 1]
        key_docs = source.astype(jnp.float32)
        column = block * LANES + lax.broadcasted_iota(jnp.int32, (LANES, LANES), 1)
        for q in range(lane_tiles):
            row = q * LANES + lax.broadcasted_iota(jnp.int32, (LANES, LANES), 0)
            distance = row + span - column
            allowed = (
                (distance >= 0)
                & (distance < WINDOW)
                & (me * rows + column - span >= 0)
                & (query_docs[q] == key_docs)
            )
            bias[q * LANES : (q + 1) * LANES, block * LANES : (block + 1) * LANES] = jnp.where(
                allowed, 0.0, MASK_FLOOR
            )
    forward_one(2)
    forward_two(0)
    forward_two(1)
    for n in range(len(shards)):
        local(n).wait()
    arrived(0)
    arrived(1)
    key_raw = r.key_raw
    key_raw[...] = dot(normed_in[...], full.key[...])
    all_keys[span : span + rows] = rotate(
        key_raw[...], gain(5, head_dim), r.cos[...], r.sin[...]
    ).astype(jnp.bfloat16)
    all_values[span : span + rows] = dot(normed_in[...], full.value[...]).astype(jnp.bfloat16)
    shift_start([0, 1])
    for i in range(5, len(items)):
        first(i).start()
    forward_one(3)
    forward_two(2)
    arrived(2)
    query_raw, queries = r.query_raw, r.queries

    @pl.loop(0, heads)
    def _(h):
        at = lane_block(h, head_dim)
        raw = dot(normed_in[...], full.query[:, at])
        query_raw[:, at] = raw
        queries[:, at] = rotate(
            raw, gain(4, head_dim), r.cos[...], r.sin[...]
        ).astype(jnp.bfloat16)

    forward_one(4)
    forward_two(3)
    shift_arrive([0, 1])
    probs, attended = r.probs, r.attended

    def attend(h):
        at = lane_block(h, head_dim)
        scores = dot_rows(queries[:, at], all_keys[...]) * score_scale + bias[...]
        weights = jnp.exp(scores - jnp.max(scores, axis=-1, keepdims=True))
        weights = weights * (1.0 / jnp.sum(weights, axis=-1, keepdims=True))
        probs[h] = weights
        attended[:, at] = dot(weights.astype(jnp.bfloat16), all_values[...]).astype(jnp.bfloat16)

    half_heads = heads // 2
    pl.loop(0, half_heads)(attend)
    forward_one(5)
    forward_two(4)
    arrived(3)
    pl.loop(half_heads, heads)(attend)
    attn_proj, resid, normed_ff = r.attn_proj, r.resid, r.normed_ff
    attn_proj[...] = dot(attended[...], full.out[...])
    forward_one(6)
    forward_two(5)
    proj = attn_proj[...]
    resid[...] = x_ref[...].astype(jnp.float32) + proj * rms_factor(proj) * (1.0 + gain(1))
    res = resid[...]
    normed_ff[...] = (res * rms_factor(res) * (1.0 + gain(2))).astype(jnp.bfloat16)
    slope, act, hidden = r.slope, r.act, r.hidden
    ff_block = 512

    def expand(j):
        at = lane_block(j, ff_block)
        gate = dot(normed_ff[...], full.gate[:, at])
        up = dot(normed_ff[...], full.up[:, at])
        square = gate * gate
        tanh = jnp.tanh(GELU_SCALE * (gate + GELU_CUBE * (square * gate)))
        below = 0.5 * (1.0 + tanh)
        value = gate * below
        slope[:, at] = up * (
            below
            + (0.5 * GELU_SCALE) * gate * (1.0 - tanh * tanh) * (1.0 + 3.0 * GELU_CUBE * square)
        )
        act[:, at] = value
        hidden[:, at] = (value * up).astype(jnp.bfloat16)

    arrived(4)
    forward_one(7)
    forward_two(6)
    arrived(5)
    pl.loop(0, half_ff // ff_block)(expand)
    forward_one(8)
    forward_two(7)
    arrived(6)
    forward_one(9)
    forward_two(8)
    arrived(7)
    pl.loop(half_ff // ff_block, ff // ff_block)(expand)
    down_rows = shards[6].shape[0]
    ff_proj = r.ff_proj
    mine = lane_block(y, down_rows)
    ff_proj[...] = dot(hidden[:, mine], full.down[mine, :])
    forward_two(9)
    arrived(8)
    arrived(9)
    theirs = lane_block(1 - y, down_rows)
    proj = ff_proj[...] + dot(hidden[:, theirs], full.down[theirs, :])
    r.layer_out[...] = (
        resid[...] + proj * rms_factor(proj) * (1.0 + gain(3))
    ).astype(jnp.bfloat16)
    grad_gains = r.grad_gains
    grad_gains[...] = jnp.zeros_like(grad_gains)
    grad_ff_proj = r.grad_ff_proj
    grad_proj, grad_gain = rms_pull(proj, gain(3), cot_ref[...].astype(jnp.float32))
    grad_gains[3:4, :] = grad_gain
    grad_ff_proj[...] = grad_proj.astype(jnp.bfloat16)

    grad_gate, grad_up, accum = r.grad_gate, r.grad_up, ff_proj
    grad_resid, grad_attn_proj = resid, r.grad_attn_proj
    grad_keys, grad_values, grad_query = r.grad_keys, r.grad_values, r.grad_query
    grad_kv, back_send, back_recv = r.grad_kv, r.back_send, r.back_recv

    def task_hidden(j):
        at = lane_block(j, ff_block)
        grad_hidden = dot_rows(grad_ff_proj[...], full.down[at, :])
        grad_gate[:, at] = (grad_hidden * slope[:, at]).astype(jnp.bfloat16)
        grad_up[:, at] = (grad_hidden * act[:, at]).astype(jnp.bfloat16)

    def task_normed_ff(j):
        at = lane_block(j, ff_block)
        accum[...] += dot_rows(grad_gate[:, at], full.gate[:, at]) + dot_rows(
            grad_up[:, at], full.up[:, at]
        )

    def task_resid():
        part, grad_gain = rms_pull(resid[...], gain(2), accum[...])
        grad_gains[2:3, :] = grad_gain
        grad_resid[...] = cot_ref[...].astype(jnp.float32) + part
        grad_proj, grad_gain = rms_pull(attn_proj[...], gain(1), grad_resid[...])
        grad_gains[1:2, :] = grad_gain
        grad_attn_proj[...] = grad_proj.astype(jnp.bfloat16)
        grad_keys[...] = jnp.zeros_like(grad_keys)
        grad_values[...] = jnp.zeros_like(grad_values)

    def task_score(h):
        at = lane_block(h, head_dim)
        grad_head = dot_rows(grad_attn_proj[...], full.out[at, :]).astype(jnp.bfloat16)
        r.grad_head[...] = grad_head
        grad_soft = dot_rows(grad_head, all_values[...])
        weights = probs[h]
        inner = jnp.sum(weights * grad_soft, axis=-1, keepdims=True)
        r.grad_score[...] = (weights * (grad_soft - inner) * score_scale).astype(jnp.bfloat16)

    def task_head(h):
        at = lane_block(h, head_dim)
        grad_score = r.grad_score[...]
        grad_keys[...] += dot_tokens(grad_score, queries[:, at])
        grad_values[...] += dot_tokens(probs[h].astype(jnp.bfloat16), r.grad_head[...])
        grad_raw, grad_gain = rotate_pull(
            query_raw[:, at], gain(4, head_dim), r.cos[...], r.sin[...],
            dot(grad_score, all_keys[...]),
        )
        grad_gains[4:5, :head_dim] += grad_gain
        grad_query[:, at] = grad_raw.astype(jnp.bfloat16)

    def back_copy(k, d):
        slot = pl.ds((hops - d) * rows, rows)
        return remote(
            back_send.at[k, slot], back_recv.at[k, d - 1],
            r.back_shift_send.at[k, d - 1], r.back_shift_recv.at[k, d - 1], neighbour(-d),
        )

    def task_send_back():
        back_send[0] = grad_keys[:span].astype(jnp.bfloat16)
        back_send[1] = grad_values[:span].astype(jnp.bfloat16)
        for d in range(1, hops + 1):
            @pl.when(there(-d))
            def _(d=d):
                for k in range(2):
                    back_copy(k, d).start()

    def task_keys():
        for d in range(1, hops + 1):
            @pl.when(there(d))
            def _(d=d):
                for k in range(2):
                    back_copy(k, d).wait_recv()

            @pl.when(jnp.logical_not(there(d)))
            def _(d=d):
                for k in range(2):
                    back_recv[k, d - 1] = jnp.zeros((rows, head_dim), jnp.bfloat16)
        own_keys, own_values = grad_keys[span:], grad_values[span:]
        for d in range(1, hops + 1):
            own_keys = own_keys + back_recv[0, d - 1].astype(jnp.float32)
            own_values = own_values + back_recv[1, d - 1].astype(jnp.float32)
        grad_raw, grad_gain = rotate_pull(
            key_raw[...], gain(5, head_dim), r.cos[...], r.sin[...], own_keys
        )
        grad_gains[5:6, :head_dim] = grad_gain
        grad_kv[:, :head_dim] = grad_raw.astype(jnp.bfloat16)
        grad_kv[:, head_dim:] = own_values.astype(jnp.bfloat16)

    def task_inputs():
        grad_normed = (
            dot_rows(grad_query[...], full.query[...])
            + dot_rows(grad_kv[:, :head_dim], full.key[...])
            + dot_rows(grad_kv[:, head_dim:], full.value[...])
        )
        part, grad_gain = rms_pull(x_ref[...].astype(jnp.float32), gain(0), grad_normed)
        grad_gains[0:1, :] = grad_gain
        r.grad_inputs[...] = grad_resid[...] + part
        grad_gains[...] = grad_gains[...].astype(jnp.bfloat16).astype(jnp.float32)

    gain_in, gain_steps, gain_sums = r.gain_in, r.gain_steps, r.gain_sums

    def gain_copy(step):
        target = ([sibling, across, beside] + line)[step]
        src = grad_gains if step == 0 else gain_steps.at[min(step, 3) - 1]
        return remote(src, gain_in.at[step], r.send_gain.at[step], r.recv_gain.at[step], target)

    def task_gain(step):
        if step == 0:
            gain_copy(0).start()
        elif step <= 3:
            gain_copy(step - 1).wait_recv()
            before = grad_gains[...] if step == 1 else gain_steps[step - 2]
            gain_steps[step - 1] = before + gain_in[step - 1]
            if step < 3:
                gain_copy(step).start()
            else:
                for d in range(1, depth):
                    gain_copy(2 + d).start()
        else:
            total = gain_steps[2]
            for d in range(1, depth):
                gain_copy(2 + d).wait_recv()
                total = total + gain_in[2 + d]
            gain_sums[...] = total

    blocks = ff // ff_block
    accum[...] = jnp.zeros_like(accum)

    def tasks(t):
        @pl.when(t < blocks)
        def _():
            task_hidden(t)

        @pl.when((t >= 1) & (t <= blocks))
        def _():
            task_normed_ff(t - 1)

        at = blocks + 1
        pl.when(t == at)(task_resid)
        at += 1
        last = at + 2 * heads - 1

        @pl.when((t >= at) & (t <= last) & ((t - at) % 2 == 0))
        def _(at=at):
            task_score((t - at) // 2)

        @pl.when((t >= at) & (t <= last) & ((t - at) % 2 == 1))
        def _(at=at):
            task_head((t - at) // 2)

        pl.when(t == last)(task_send_back)
        pl.when(t == last + 2)(task_keys)
        pl.when(t == last + 3)(task_inputs)
        for step in range(5):
            pl.when(t == last + 4 + step)(functools.partial(task_gain, step))

    lefts = (hidden, normed_ff, normed_ff, attended, normed_in, normed_in)
    rights = (grad_ff_proj, grad_gate, grad_up, grad_attn_proj, grad_query, grad_kv)
    reduce_steps(r, lefts, rights, dim, depth, x, core, z, y, sibling, beside, across, line, tasks)

    gain_gather().wait_send()
    for i in range(len(items)):
        first(i).wait_send()
        second(i).wait_send()
        third(i, x, 2).wait_send()
        third(i, 1 - x, 3).wait_send()
    for d in range(1, hops + 1):
        @pl.when(there(d))
        def _(d=d):
            for k in range(3):
                shift_copy(k, d).wait_send()

        @pl.when(there(-d))
        def _(d=d):
            for k in range(2):
                back_copy(k, d).wait_send()
    for step in range(2 + depth):
        gain_copy(step).wait_send()


def term_groups(lefts, rights, dim, depth):
    groups = []
    for left, right in zip(lefts, rights):
        columns = right.shape[1]
        by_columns = columns % (depth * LANES) == 0
        piece = dim // 8 * LANES
        if by_columns:
            chunks = columns // (depth * LANES)
        else:
            chunks = left.shape[1] * columns // (8 * depth * piece)
        groups.append((left, right, by_columns, chunks))
    return groups


def reduce_steps(
    r, lefts, rights, dim, depth, x, core, z, y, sibling, beside, across, line, tasks
):
    terms, out = r.terms, r.summed
    from_core, from_across, from_beside, from_line = (
        r.from_core, r.from_across, r.from_beside, r.from_line
    )
    chunks = terms.shape[0]
    piece_rows = terms.shape[5]

    def to_core(c):
        send, recv = r.sem_core
        return remote(terms.at[c, 1 - core], from_core.at[c], send.at[c], recv.at[c], sibling)

    def to_across(c):
        send, recv = r.sem_across
        return remote(from_core.at[c, 1 - y], from_across.at[c], send.at[c], recv.at[c], across)

    def to_beside(c):
        send, recv = r.sem_beside
        return remote(from_across.at[c, 1 - x], from_beside.at[c], send.at[c], recv.at[c], beside)

    def to_line(c, d):
        send, recv = r.sem_line
        return remote(
            from_beside.at[c, lax.rem(z + d, depth)], from_line.at[c, d - 1],
            send.at[c, d - 1], recv.at[c, d - 1], line[d - 1],
        )

    def along_line(c, d, arrival=False):
        send, recv = r.sem_zline
        block = out.at[c, core, x, lax.rem(z + depth - d, depth) if arrival else z]
        return remote(block, block, send.at[c, d - 1], recv.at[c, d - 1], line[d - 1])

    def back_beside(c, side):
        send, recv = r.sem_xback
        block = out.at[c, core, side]
        return remote(block, block, send.at[c], recv.at[c], beside)

    def back_core(c, side):
        send, recv = r.sem_back
        block = out.at[c, side]
        return remote(block, block, send.at[c], recv.at[c], sibling)

    def make_columns(left, right, at, c):
        width = depth * LANES
        block = token_dot(left[...], right[:, lane_block(at, width)])
        for side in range(2):
            for own in range(2):
                for across_x in range(2):
                    low = ((side * 2 + own) * 2 + across_x) * piece_rows
                    for place in range(depth):
                        terms[c, own, side, across_x, place] = block[
                            low : low + piece_rows, place * LANES : (place + 1) * LANES
                        ]

    def make_rows(left, right, at, c, parts):
        rows, tiles = left.shape[1] // (2 * parts), right.shape[1] // LANES
        high = rows // (4 * depth)
        for side in range(2):
            start = pl.multiple_of((side * parts + at) * rows, rows)
            block = token_dot(left[:, pl.ds(start, rows)], right[...])
            for own in range(2):
                for across_x in range(2):
                    for place in range(depth):
                        low = ((own * 2 + across_x) * depth + place) * high
                        for tile in range(tiles):
                            terms[
                                c, own, side, across_x, place, tile * high : (tile + 1) * high
                            ] = block[low : low + high, tile * LANES : (tile + 1) * LANES]

    def make(t):
        start = 0
        for left, right, by_columns, parts in term_groups(lefts, rights, dim, depth):
            @pl.when((t >= start) & (t < start + parts))
            def _(left=left, right=right, by_columns=by_columns, parts=parts, start=start):
                if by_columns:
                    make_columns(left, right, t - start, t)
                else:
                    make_rows(left, right, t - start, t, parts)
            start += parts
        to_core(t).start()

    def stage(at, action):
        @pl.when((at >= 0) & (at < chunks))
        def _():
            action(at)

    def after_core(c):
        to_core(c).wait_recv()
        from_core[c, 1 - y] = add_bf16(from_core[c, 1 - y], terms[c, core, 1 - y])
        to_across(c).start()
        from_core[c, y] = add_bf16(from_core[c, y], terms[c, core, y])

    def after_across(c):
        to_across(c).wait_recv()
        from_across[c, 1 - x] = add_bf16(from_across[c, 1 - x], from_core[c, y, 1 - x])
        to_beside(c).start()
        from_across[c, x] = add_bf16(from_across[c, x], from_core[c, y, x])

    def after_beside(c):
        to_beside(c).wait_recv()
        from_beside[c] = add_bf16(from_beside[c], from_across[c, x])
        for d in range(1, depth):
            to_line(c, d).start()

    def after_line(c):
        total = from_beside[c, z].astype(jnp.float32)
        for d in range(1, depth):
            to_line(c, d).wait_recv()
            total = total + from_line[c, d - 1].astype(jnp.float32)
        out[c, core, x, z] = total.astype(jnp.bfloat16)
        for d in range(1, depth):
            along_line(c, d).start()

    def after_zline(c):
        for d in range(1, depth):
            along_line(c, d, True).wait_recv()
        back_beside(c, x).start()

    def after_xback(c):
        back_beside(c, 1 - x).wait_recv()
        back_core(c, core).start()

    actions = [make, after_core, after_across, after_beside, after_line, after_zline, after_xback]

    @pl.loop(0, chunks + len(actions) - 1)
    def _(t):
        for lag, action in enumerate(actions):
            stage(t - lag, action)
        tasks(t)

    @pl.loop(0, chunks)
    def _(c):
        back_core(c, 1 - core).wait_recv()
        to_core(c).wait_send()
        to_across(c).wait_send()
        to_beside(c).wait_send()
        for d in range(1, depth):
            to_line(c, d).wait_send()
            along_line(c, d).wait_send()
        back_beside(c, x).wait_send()
        back_core(c, core).wait_send()


def run_layer(x, cotangent, docs, cos_table, sin_table, gains_own, weights):
    rows, dim = x.shape
    depth = lax.axis_size("seq") // 4
    head_dim = weights.key.shape[1]
    inner = weights.query.shape[1]
    heads = inner // head_dim
    ff = weights.gate.shape[1]
    hops = WINDOW // rows
    keys = (hops + 1) * rows
    bf16, f32 = jnp.bfloat16, jnp.float32
    dma = pltpu.SemaphoreType.DMA
    chunks = (2 * inner * dim + 2 * dim * head_dim + 3 * dim * ff) // (dim * depth * LANES)
    piece = (dim // 8, LANES)
    item_count = 10
    gain_shape = (GAIN_ROWS, dim)
    pair = Sems(dma((chunks,)), dma((chunks,)))
    lines = Sems(dma((chunks, depth - 1)), dma((chunks, depth - 1)))
    fulls = [pltpu.VMEM((2 * w.shape[0], w.shape[1]), bf16) for w in weights]
    scratch = dict(
        gains_other=pltpu.VMEM(gain_shape, f32),
        gains=pltpu.VMEM(gain_shape, f32),
        halo_docs=pltpu.VMEM((hops,) + docs.shape, docs.dtype),
        bias=pltpu.VMEM((rows, keys), f32),
        normed_in=pltpu.VMEM((rows, dim), bf16),
        key_raw=pltpu.VMEM((rows, head_dim), f32),
        query_raw=pltpu.VMEM((rows, inner), f32),
        queries=pltpu.VMEM((rows, inner), bf16),
        all_keys=pltpu.VMEM((keys, head_dim), bf16),
        all_values=pltpu.VMEM((keys, head_dim), bf16),
        probs=pltpu.VMEM((heads, rows, keys), f32),
        attended=pltpu.VMEM((rows, inner), bf16),
        attn_proj=pltpu.VMEM((rows, dim), f32),
        resid=pltpu.VMEM((rows, dim), f32),
        normed_ff=pltpu.VMEM((rows, dim), bf16),
        slope=pltpu.VMEM((rows, ff), f32),
        act=pltpu.VMEM((rows, ff), f32),
        hidden=pltpu.VMEM((rows, ff), bf16),
        ff_proj=pltpu.VMEM((rows, dim), f32),
        grad_ff_proj=pltpu.VMEM((rows, dim), bf16),
        grad_gains=pltpu.VMEM(gain_shape, f32),
        grad_gate=pltpu.VMEM((rows, ff), bf16),
        grad_up=pltpu.VMEM((rows, ff), bf16),
        grad_attn_proj=pltpu.VMEM((rows, dim), bf16),
        grad_head=pltpu.VMEM((rows, head_dim), bf16),
        grad_score=pltpu.VMEM((rows, keys), bf16),
        grad_keys=pltpu.VMEM((keys, head_dim), f32),
        grad_values=pltpu.VMEM((keys, head_dim), f32),
        grad_query=pltpu.VMEM((rows, inner), bf16),
        grad_kv=pltpu.VMEM((rows, 2 * head_dim), bf16),
        back_send=pltpu.VMEM((2, hops * rows, head_dim), bf16),
        back_recv=pltpu.VMEM((2, hops, rows, head_dim), bf16),
        terms=pltpu.VMEM((chunks, 2, 2, 2, depth) + piece, bf16),
        from_core=pltpu.VMEM((chunks, 2, 2, depth) + piece, bf16),
        from_across=pltpu.VMEM((chunks, 2, depth) + piece, bf16),
        from_beside=pltpu.VMEM((chunks, depth) + piece, bf16),
        from_line=pltpu.VMEM((chunks, depth - 1) + piece, bf16),
        gain_in=pltpu.VMEM((2 + depth,) + gain_shape, f32),
        gain_steps=pltpu.VMEM((3,) + gain_shape, f32),
        gain_gather_sems=dma((2,)),
        own_sems=dma((len(weights),)),
        g_send=dma((4, item_count)),
        g_recv=dma((4, item_count)),
        shift_send=dma((3, hops)),
        shift_recv=dma((3, hops)),
        back_shift_send=dma((2, hops)),
        back_shift_recv=dma((2, hops)),
        send_gain=dma((2 + depth,)),
        recv_gain=dma((2 + depth,)),
        sem_core=pair,
        sem_across=pair,
        sem_beside=pair,
        sem_xback=pair,
        sem_back=pair,
        sem_line=lines,
        sem_zline=lines,
    )
    vmem = pl.BlockSpec(memory_space=pltpu.VMEM)
    return pl.pallas_call(
        functools.partial(layer_kernel, tuple(scratch)),
        out_shape=[
            jax.ShapeDtypeStruct((rows, dim), bf16),
            jax.ShapeDtypeStruct((rows, dim), f32),
            jax.ShapeDtypeStruct((chunks, 2, 2, depth) + piece, bf16),
            jax.ShapeDtypeStruct(gain_shape, f32),
        ],
        in_specs=[vmem] * 6 + [pl.BlockSpec(memory_space=pl.ANY)] * len(weights),
        out_specs=[vmem] * 4,
        scratch_shapes=fulls + list(scratch.values()),
        compiler_params=pltpu.CompilerParams(
            collective_id=1, has_side_effects=True, vmem_limit_bytes=67043328
        ),
        name="layer",
    )(x, cotangent, docs, cos_table, sin_table, gains_own, *weights)


def finish_kernel(plan, count, summed, layer_in, inputs_in, *refs):
    outs, layer_out, grad_inputs = refs[:count], refs[count], refs[count + 1]
    stages = refs[count + 2 : 2 * count + 2]
    chunk_sems, side_sems = refs[2 * count + 2 :]
    depth, rows = summed.shape[3], summed.shape[4]
    sides = [
        pltpu.make_async_copy(layer_in, layer_out, side_sems.at[0]),
        pltpu.make_async_copy(inputs_in, grad_inputs, side_sems.at[1]),
    ]
    for copy in sides:
        copy.start()

    def copies(group, at):
        outputs, by_columns, start, parts = group
        if len(outputs) > 1:
            return [
                pltpu.make_async_copy(stages[k], outs[k], chunk_sems.at[start + n])
                for n, k in enumerate(outputs)
            ]
        stage, out = stages[outputs[0]], outs[outputs[0]]
        if by_columns:
            view = (slice(None), lane_block(at, depth * LANES))
        else:
            high = stage.shape[0] // parts
            view = (pl.ds(pl.multiple_of(at * high, high), high),)
        return [pltpu.make_async_copy(stage.at[view], out.at[view], chunk_sems.at[start + at])]

    def convert(group, at):
        outputs, by_columns, start, parts = group
        stage = stages[outputs[0]]
        for core in range(2):
            for x in range(2):
                for z in range(depth):
                    piece = summed[start + at, core, x, z].astype(jnp.float32)
                    if by_columns:
                        low = (core * 2 + x) * rows
                        if len(outputs) > 1:
                            wide = stage.shape[1]
                            stage = stages[outputs[z * LANES // wide]]
                            place = pl.ds(z * LANES % wide, LANES)
                        else:
                            place = pl.ds(
                                pl.multiple_of(at * depth * LANES + z * LANES, LANES), LANES
                            )
                        stage[low : low + rows, place] = piece
                    else:
                        tiles = stage.shape[1] // LANES
                        high = rows // tiles
                        block = stage.shape[0] // parts
                        low = pl.multiple_of(
                            at * block + ((core * 2 + x) * depth + z) * high, high
                        )
                        for tile in range(tiles):
                            stage[pl.ds(low, high), tile * LANES : (tile + 1) * LANES] = piece[
                                tile * high : (tile + 1) * high
                            ]
        for copy in copies(group, at):
            copy.start()

    for group in plan:
        if group[3] == 1:
            convert(group, 0)
        else:
            pl.loop(0, group[3])(functools.partial(convert, group))
    for group in plan:
        for at in range(group[3]):
            for copy in copies(group, at):
                copy.wait()
    for copy in sides:
        copy.wait()


def finish(summed, layer_out, grad_inputs, shapes):
    chunks, _, _, depth, rows, lanes = summed.shape
    width = depth * lanes
    plan, start, index = [], 0, 0
    while index < len(shapes):
        high, wide = shapes[index]
        together = max(1, width // wide) if wide <= width and width % wide == 0 else 1
        by_columns = (wide * together) % width == 0
        if by_columns:
            parts = wide * together // width
        else:
            parts = high * wide // (4 * depth * rows * lanes)
        plan.append((list(range(index, index + together)), by_columns, start, parts))
        start += parts
        index += together
    vmem, anywhere = pl.BlockSpec(memory_space=pltpu.VMEM), pl.BlockSpec(memory_space=pl.ANY)
    results = [jax.ShapeDtypeStruct(shape, jnp.float32) for shape in shapes]
    return pl.pallas_call(
        functools.partial(finish_kernel, plan, len(shapes)),
        out_shape=results
        + [jax.ShapeDtypeStruct(a.shape, a.dtype) for a in (layer_out, grad_inputs)],
        in_specs=[vmem] * 3,
        out_specs=[anywhere] * (len(shapes) + 2),
        scratch_shapes=[pltpu.VMEM(shape, jnp.float32) for shape in shapes]
        + [pltpu.SemaphoreType.DMA((chunks + len(shapes),)), pltpu.SemaphoreType.DMA((2,))],
        compiler_params=pltpu.CompilerParams(vmem_limit_bytes=40 * 2**20),
        name="finish",
    )(summed, layer_out, grad_inputs)


def pack_gains(small, dim):
    me = lax.axis_index("wshard")
    row_at = lax.broadcasted_iota(jnp.int32, (GAIN_ROWS, dim), 0)
    packed = jnp.zeros((GAIN_ROWS, dim), jnp.float32)
    for row, vec in enumerate(small):
        n = vec.shape[0]
        vec = vec.astype(jnp.float32)
        spread = jnp.where(me == 0, jnp.pad(vec, (0, dim - n)), jnp.pad(vec, (n, dim - 2 * n)))
        wide = lax.broadcast_in_dim(spread, (GAIN_ROWS, dim), (1,))
        packed = jnp.where(row_at == row, wide, packed)
    return packed


def per_device(
    inputs, doc_ids, w_query, w_key, w_value, w_out, w_gate, w_up, w_down,
    gain_in, gain_attn_post, gain_ff_pre, gain_ff_post, gain_query, gain_key, cotangent,
):
    rows, dim = inputs.shape
    small = (gain_in, gain_attn_post, gain_ff_pre, gain_ff_post, gain_query, gain_key)
    start_row = lax.axis_index(("seq", "wshard")) * rows
    cos_table, sin_table = rope_tables(
        start_row + jnp.arange(rows, dtype=jnp.int32), w_key.shape[1]
    )
    layer_out, grad_inputs, summed, gain_sums = run_layer(
        inputs, cotangent, doc_ids.reshape(-1, LANES), cos_table, sin_table,
        pack_gains(small, dim), Weights(w_key, w_value, w_query, w_out, w_gate, w_up, w_down),
    )
    order = (w_down, w_gate, w_up, w_out, w_query, w_key, w_value)
    results = finish(summed, layer_out, grad_inputs, [w.shape for w in order])
    sum_down, sum_gate, sum_up, sum_out, sum_query, sum_key, sum_value = results[:7]
    layer_out, grad_inputs = results[7:]
    me = lax.axis_index("wshard")
    gain_outs = []
    for row, vec in enumerate(small):
        n = vec.shape[0]
        gain_outs.append(jnp.where(me == 0, gain_sums[row, :n], gain_sums[row, n : 2 * n]))
    return (
        layer_out, grad_inputs, sum_query, sum_key, sum_value, sum_out, sum_gate, sum_up, sum_down,
    ) + tuple(gain_outs)


def per_device_general(
    inputs,
    doc_ids,
    w_query,
    w_key,
    w_value,
    w_out,
    w_gate,
    w_up,
    w_down,
    gain_in,
    gain_attn_post,
    gain_ff_pre,
    gain_ff_post,
    gain_query,
    gain_key,
    cotangent,
):
    gathered = (
        lax.all_gather(w_query, "wshard", axis=0, tiled=True),
        lax.all_gather(w_key, "wshard", axis=0, tiled=True),
        lax.all_gather(w_value, "wshard", axis=0, tiled=True),
        lax.all_gather(w_out, "wshard", axis=0, tiled=True),
        lax.all_gather(w_gate, "wshard", axis=0, tiled=True),
        lax.all_gather(w_up, "wshard", axis=0, tiled=True),
        lax.all_gather(w_down, "wshard", axis=0, tiled=True),
        lax.all_gather(gain_in, "wshard", axis=0, tiled=True),
        lax.all_gather(gain_attn_post, "wshard", axis=0, tiled=True),
        lax.all_gather(gain_ff_pre, "wshard", axis=0, tiled=True),
        lax.all_gather(gain_ff_post, "wshard", axis=0, tiled=True),
        lax.all_gather(gain_query, "wshard", axis=0, tiled=True),
        lax.all_gather(gain_key, "wshard", axis=0, tiled=True),
    )
    full_query, full_key, full_value, full_out, full_gate, full_up, full_down = gathered[:7]
    in_gain, attn_post_gain, ff_pre_gain, ff_post_gain, query_gain, key_gain = [
        g.astype(jnp.float32) for g in gathered[7:]
    ]
    row_count = inputs.shape[0]
    head_dim = full_key.shape[1]
    head_count = full_query.shape[1] // head_dim
    score_scale = head_dim ** (-0.5)
    start_row = lax.axis_index(("seq", "wshard")) * row_count
    query_pos = start_row + jnp.arange(row_count, dtype=jnp.int32)
    cos_table, sin_table = rope_tables(query_pos, head_dim)
    x_float = inputs.astype(jnp.float32)
    normed_in = rms_gain(x_float, in_gain).astype(jnp.bfloat16)
    query_raw = jnp.dot(normed_in, full_query, preferred_element_type=jnp.float32).reshape(
        row_count, head_count, head_dim
    )
    key_raw = jnp.dot(normed_in, full_key, preferred_element_type=jnp.float32)[:, None, :]
    values = jnp.dot(normed_in, full_value, preferred_element_type=jnp.float32).astype(jnp.bfloat16)
    queries = norm_rope(query_raw, query_gain, cos_table, sin_table).astype(jnp.bfloat16)
    key_rot = norm_rope(key_raw, key_gain, cos_table, sin_table)[:, 0].astype(jnp.bfloat16)
    sent_rows = min(WINDOW, row_count)
    hop_count = WINDOW // sent_rows
    outgoing = (key_rot, values, doc_ids)
    halo_keys = []
    halo_values = []
    halo_docs = []
    for distance in range(hop_count, 0, -1):
        arrived = from_behind((outgoing[0], outgoing[1], outgoing[2]), ("seq", "wshard"), distance)
        halo_keys.append(arrived[0])
        halo_values.append(arrived[1])
        halo_docs.append(arrived[2])
    all_keys = jnp.concatenate(halo_keys + [key_rot], 0)
    all_values = jnp.concatenate(halo_values + [values], 0)
    all_docs = jnp.concatenate(halo_docs + [doc_ids], 0)
    key_pos = start_row - WINDOW + jnp.arange(WINDOW + row_count, dtype=jnp.int32)
    allowed = window_mask(query_pos, key_pos, doc_ids, all_docs)
    scores = masked_scores(queries, all_keys, allowed, score_scale)
    row_peak = jnp.max(scores, axis=-1, keepdims=True)
    row_total = jnp.sum(
        jnp.where(allowed[None], jnp.exp(scores - row_peak), 0.0), axis=-1, keepdims=True
    )
    log_total = row_peak + jnp.log(row_total)
    soft = jnp.where(allowed[None], jnp.exp(scores - log_total), 0.0).astype(jnp.bfloat16)
    attended = jnp.einsum("hqk,kd->qhd", soft, all_values, preferred_element_type=jnp.float32)
    attended = attended.reshape(row_count, head_count * head_dim).astype(jnp.bfloat16)
    attn_proj = jnp.dot(attended, full_out, preferred_element_type=jnp.float32)
    resid = x_float + rms_gain(attn_proj, attn_post_gain)
    normed_ff = rms_gain(resid, ff_pre_gain).astype(jnp.bfloat16)
    gate_pre = jnp.dot(normed_ff, full_gate, preferred_element_type=jnp.float32)
    up_pre = jnp.dot(normed_ff, full_up, preferred_element_type=jnp.float32)
    hidden = geglu(gate_pre, up_pre).astype(jnp.bfloat16)
    ff_proj = jnp.dot(hidden, full_down, preferred_element_type=jnp.float32)
    layer_out = (resid + rms_gain(ff_proj, ff_post_gain)).astype(jnp.bfloat16)
    grad_top = cotangent.astype(jnp.float32)
    _, pullback = jax.vjp(rms_gain, ff_proj, ff_post_gain)
    grad_ff_proj, grad_gain_ff_post = pullback(grad_top)
    grad_ff_proj = grad_ff_proj.astype(jnp.bfloat16)
    grad_w_down = weight_grad(hidden, grad_ff_proj)
    grad_hidden = lax.dot_general(
        grad_ff_proj, full_down, (((1,), (1,)), ((), ())), preferred_element_type=jnp.float32
    )
    _, pullback = jax.vjp(geglu, gate_pre, up_pre)
    grad_gate, grad_up = pullback(grad_hidden)
    grad_gate = grad_gate.astype(jnp.bfloat16)
    grad_up = grad_up.astype(jnp.bfloat16)
    grad_w_gate = weight_grad(normed_ff, grad_gate)
    grad_w_up = weight_grad(normed_ff, grad_up)
    grad_normed_ff = lax.dot_general(
        grad_gate, full_gate, (((1,), (1,)), ((), ())), preferred_element_type=jnp.float32
    )
    grad_normed_ff = grad_normed_ff + lax.dot_general(
        grad_up, full_up, (((1,), (1,)), ((), ())), preferred_element_type=jnp.float32
    )
    _, pullback = jax.vjp(rms_gain, resid, ff_pre_gain)
    grad_resid_part, grad_gain_ff_pre = pullback(grad_normed_ff)
    grad_resid = grad_top + grad_resid_part
    ff_gradients = (grad_w_gate, grad_w_up, grad_w_down, grad_gain_ff_pre, grad_gain_ff_post)
    ff_parts = (
        lax.psum_scatter(
            ff_gradients[0].astype(jnp.bfloat16), "wshard", scatter_dimension=0, tiled=True
        ).astype(jnp.float32),
        lax.psum_scatter(
            ff_gradients[1].astype(jnp.bfloat16), "wshard", scatter_dimension=0, tiled=True
        ).astype(jnp.float32),
        lax.psum_scatter(
            ff_gradients[2].astype(jnp.bfloat16), "wshard", scatter_dimension=0, tiled=True
        ).astype(jnp.float32),
        lax.psum_scatter(
            ff_gradients[3].astype(jnp.bfloat16), "wshard", scatter_dimension=0, tiled=True
        ).astype(jnp.float32),
        lax.psum_scatter(
            ff_gradients[4].astype(jnp.bfloat16), "wshard", scatter_dimension=0, tiled=True
        ).astype(jnp.float32),
    )
    ff_reduced = (
        lax.psum(ff_parts[0].astype(jnp.bfloat16), "seq").astype(jnp.float32),
        lax.psum(ff_parts[1].astype(jnp.bfloat16), "seq").astype(jnp.float32),
        lax.psum(ff_parts[2].astype(jnp.bfloat16), "seq").astype(jnp.float32),
        lax.psum(ff_parts[3].astype(jnp.bfloat16), "seq").astype(jnp.float32),
        lax.psum(ff_parts[4].astype(jnp.bfloat16), "seq").astype(jnp.float32),
    )
    _, pullback = jax.vjp(rms_gain, attn_proj, attn_post_gain)
    grad_attn_proj, grad_gain_attn_post = pullback(grad_resid)
    grad_attn_proj = grad_attn_proj.astype(jnp.bfloat16)
    grad_w_out = weight_grad(attended, grad_attn_proj)
    grad_attended = lax.dot_general(
        grad_attn_proj, full_out, (((1,), (1,)), ((), ())), preferred_element_type=jnp.float32
    ).astype(jnp.bfloat16)
    grad_heads = grad_attended.reshape(row_count, head_count, head_dim)
    again_scores = masked_scores(queries, all_keys, allowed, score_scale)
    probs = jnp.where(allowed[None], jnp.exp(again_scores - log_total), 0.0)
    grad_soft = jnp.einsum(
        "qhd,kd->hqk", grad_heads, all_values, preferred_element_type=jnp.float32
    )
    row_inner = jnp.sum(probs * grad_soft, axis=-1, keepdims=True)
    grad_score = (probs * (grad_soft - row_inner) * score_scale).astype(jnp.bfloat16)
    grad_queries = jnp.einsum(
        "hqk,kd->qhd", grad_score, all_keys, preferred_element_type=jnp.float32
    )
    grad_keys_all = jnp.einsum(
        "hqk,qhd->kd", grad_score, queries, preferred_element_type=jnp.float32
    )
    grad_values_all = jnp.einsum(
        "hqk,qhd->kd", probs.astype(jnp.bfloat16), grad_heads, preferred_element_type=jnp.float32
    )
    back_keys = jnp.zeros((sent_rows, head_dim), jnp.float32)
    back_values = jnp.zeros((sent_rows, head_dim), jnp.float32)
    for piece_index in range(hop_count):
        distance = hop_count - piece_index
        piece_start = piece_index * sent_rows
        arrived = (
            from_behind(
                grad_keys_all[piece_start : piece_start + sent_rows].astype(jnp.bfloat16),
                ("seq", "wshard"),
                -distance,
            ).astype(jnp.float32),
            from_behind(
                grad_values_all[piece_start : piece_start + sent_rows].astype(jnp.bfloat16),
                ("seq", "wshard"),
                -distance,
            ).astype(jnp.float32),
        )
        back_keys = back_keys + arrived[0]
        back_values = back_values + arrived[1]
    own_keys = grad_keys_all[WINDOW:]
    own_values = grad_values_all[WINDOW:]
    split_row = row_count - sent_rows
    grad_keys = jnp.concatenate([own_keys[:split_row], own_keys + back_keys], 0)
    grad_values = jnp.concatenate([own_values[:split_row], own_values + back_values], 0).astype(
        jnp.bfloat16
    )

    def query_path(tensor, gain_vec):
        return norm_rope(tensor, gain_vec, cos_table, sin_table)

    _, pullback = jax.vjp(query_path, query_raw, query_gain)
    grad_query_raw, grad_gain_query = pullback(grad_queries)
    _, pullback = jax.vjp(query_path, key_raw, key_gain)
    grad_key_raw, grad_gain_key = pullback(grad_keys[:, None, :])
    grad_query_raw = grad_query_raw.reshape(row_count, head_count * head_dim).astype(jnp.bfloat16)
    grad_key_raw = grad_key_raw[:, 0].astype(jnp.bfloat16)
    grad_w_query = weight_grad(normed_in, grad_query_raw)
    grad_w_key = weight_grad(normed_in, grad_key_raw)
    grad_w_value = weight_grad(normed_in, grad_values)
    grad_normed_in = lax.dot_general(
        grad_query_raw, full_query, (((1,), (1,)), ((), ())), preferred_element_type=jnp.float32
    )
    grad_normed_in = grad_normed_in + lax.dot_general(
        grad_key_raw, full_key, (((1,), (1,)), ((), ())), preferred_element_type=jnp.float32
    )
    grad_normed_in = grad_normed_in + lax.dot_general(
        grad_values, full_value, (((1,), (1,)), ((), ())), preferred_element_type=jnp.float32
    )
    _, pullback = jax.vjp(rms_gain, x_float, in_gain)
    grad_input_part, grad_gain_in = pullback(grad_normed_in)
    grad_inputs = grad_resid + grad_input_part
    attn_gradients = (
        grad_w_query,
        grad_w_key,
        grad_w_value,
        grad_w_out,
        grad_gain_in,
        grad_gain_attn_post,
        grad_gain_query,
        grad_gain_key,
    )
    attn_parts = (
        lax.psum_scatter(
            attn_gradients[0].astype(jnp.bfloat16), "wshard", scatter_dimension=0, tiled=True
        ).astype(jnp.float32),
        lax.psum_scatter(
            attn_gradients[1].astype(jnp.bfloat16), "wshard", scatter_dimension=0, tiled=True
        ).astype(jnp.float32),
        lax.psum_scatter(
            attn_gradients[2].astype(jnp.bfloat16), "wshard", scatter_dimension=0, tiled=True
        ).astype(jnp.float32),
        lax.psum_scatter(
            attn_gradients[3].astype(jnp.bfloat16), "wshard", scatter_dimension=0, tiled=True
        ).astype(jnp.float32),
        lax.psum_scatter(
            attn_gradients[4].astype(jnp.bfloat16), "wshard", scatter_dimension=0, tiled=True
        ).astype(jnp.float32),
        lax.psum_scatter(
            attn_gradients[5].astype(jnp.bfloat16), "wshard", scatter_dimension=0, tiled=True
        ).astype(jnp.float32),
        lax.psum_scatter(
            attn_gradients[6].astype(jnp.bfloat16), "wshard", scatter_dimension=0, tiled=True
        ).astype(jnp.float32),
        lax.psum_scatter(
            attn_gradients[7].astype(jnp.bfloat16), "wshard", scatter_dimension=0, tiled=True
        ).astype(jnp.float32),
    )
    attn_reduced = (
        lax.psum(attn_parts[0].astype(jnp.bfloat16), "seq").astype(jnp.float32),
        lax.psum(attn_parts[1].astype(jnp.bfloat16), "seq").astype(jnp.float32),
        lax.psum(attn_parts[2].astype(jnp.bfloat16), "seq").astype(jnp.float32),
        lax.psum(attn_parts[3].astype(jnp.bfloat16), "seq").astype(jnp.float32),
        lax.psum(attn_parts[4].astype(jnp.bfloat16), "seq").astype(jnp.float32),
        lax.psum(attn_parts[5].astype(jnp.bfloat16), "seq").astype(jnp.float32),
        lax.psum(attn_parts[6].astype(jnp.bfloat16), "seq").astype(jnp.float32),
        lax.psum(attn_parts[7].astype(jnp.bfloat16), "seq").astype(jnp.float32),
    )
    reduced = (
        attn_reduced[0],
        attn_reduced[1],
        attn_reduced[2],
        attn_reduced[3],
        ff_reduced[0],
        ff_reduced[1],
        ff_reduced[2],
        attn_reduced[4],
        attn_reduced[5],
        ff_reduced[3],
        ff_reduced[4],
        attn_reduced[6],
        attn_reduced[7],
    )
    return (layer_out, grad_inputs) + tuple(reduced)


def solution(mesh):
    routed = mesh.shape["wshard"] == 2 and mesh.shape["seq"] == 16
    return jax.shard_map(
        per_device if routed else per_device_general,
        mesh=mesh,
        in_specs=(
            P(("seq", "wshard"), None),
            P(("seq", "wshard")),
            P("wshard", None),
            P("wshard", None),
            P("wshard", None),
            P("wshard", None),
            P("wshard", None),
            P("wshard", None),
            P("wshard", None),
            P("wshard"),
            P("wshard"),
            P("wshard"),
            P("wshard"),
            P("wshard"),
            P("wshard"),
            P(("seq", "wshard"), None),
        ),
        out_specs=(
            P(("seq", "wshard"), None),
            P(("seq", "wshard"), None),
            P("wshard", None),
            P("wshard", None),
            P("wshard", None),
            P("wshard", None),
            P("wshard", None),
            P("wshard", None),
            P("wshard", None),
            P("wshard"),
            P("wshard"),
            P("wshard"),
            P("wshard"),
            P("wshard"),
            P("wshard"),
        ),
        check_vma=False,
    )
```

time: 273 us -> 180 us (0.66)
  matrix products: 45.7 us -> 0 us
  Pallas kernels: 183 us -> 165 us
  local copies, waits for them, and re-layouts: 22 us -> 4.64 us
  other arithmetic: 19.5 us -> 9.09 us
    dot_general x20 -> x0, matrix products: 45.7 us -> none  [the longest x1 8.3 us: per_device(): jnp.einsum('hqk,kd->qhd', grad_score, all_keys, preferred_element_type=jn...]
    pallas_call x5 -> x2, Pallas kernels: 183 us -> 165 us  [the longest x1 161 us: run_layer(): pl.pallas_call(functools.partial(layer_kernel, tuple(scratch)), out_shape...]
    reduce_sum x10 -> x0, other arithmetic: 6.16 us -> none  [the longest x4 2.55 us: rms_gain(): return tensor * factor * (1.0 + gain_vec)]
    concatenate x2 -> x0, local copies, waits for them, and re-layouts: 4.41 us -> none  [the longest x1 4.22 us: per_device(): jnp.concatenate(small).astype(jnp.float32).reshape(1, -1, LANES)]
    unnamed x110 -> x6, local copies, waits for them, and re-layouts: 8.67 us -> 4.64 us
    select_n x0 -> x6, other arithmetic: none -> 3.79 us  [the longest x2 2.94 us: per_device(): jnp.where(me == 0, gain_sums[row, :n], gain_sums[row, n:2 * n])]
    convert_element_type x9 -> x7, other arithmetic: 5.55 us -> 4.04 us  [the longest x6 4.04 us: pack_gains(): vec = vec.astype(jnp.float32)]
where the time goes in v1:
time: 180 us
  Pallas kernels  165 us (92%)
  other arithmetic  9.09 us (5%)
  local copies, waits for them, and re-layouts  4.64 us (3%)
    pallas_call x1, Pallas kernels, run_layer(): pl.pallas_call(functools.partial(layer_kernel, tuple(scratch)), out_shape...  161 us
    unnamed x6, local copies, waits for them, and re-layouts  4.64 us
    pallas_call x1, Pallas kernels, finish(): pl.pallas_call(functools.partial(finish_kernel, plan, len(shapes)), out_s...  4.62 us
    convert_element_type x6, other arithmetic, pack_gains(): vec = vec.astype(jnp.float32)  4.04 us

profile of v1, /device:TPU:0, one launch (start us, length us, event | category | flops | bytes accessed | tf_op | source)
XLA Modules:
  0.0 179.6 jit_solution(18240345908014777434)
XLA Ops:
  0.7 0.7 convert_element_type.43
  1.3 0.7 convert_element_type.42
  2.0 0.7 convert_element_type.47
  2.7 0.7 convert_element_type.46
  3.4 0.7 convert_element_type.45
  4.1 0.7 convert_element_type.44
  4.7 0.1 pad_select_fusion.2
  4.8 0.1 pad_select_fusion
  4.9 0.7 select_select_fusion.refs_5_
  5.6 1.2 multiply_sine_fusion
  6.8 160.5 %layer.1 = (bf16[256,640]{1,0:T(8,128)(2,1)}, f32[256,640]{1,0:T(8,128)}, bf16[17,2,2,4,80,128]{5,4,3,2,1,0:T(8,128)(2,1)}, f32[8,640]{1,0:T(8,128)}) custom-call(bf16[256,640]{1,0:T(8,128)(2,1)} %refs_0_.1, bf16[256,640]{1,0:T(8,128)(2,1)} %refs_1_.1, s32[2,128]{1,0:T(2,128)} %bitcast.5, f32[256,128]{1,0:T(8,128)} %get-tuple-element.48.refs_3_, ...), custom_call_target="tpu_custom_call" | custom-call | tf_op jit(solution)/shard_map/layer/pallas_call | solution.py:902
  167.4 1.3 fusion.5
  168.6 1.7 fusion.3
  170.3 0.0 copy-start
  170.3 2.6 %copy-done = bf16[17,2,2,4,80,128]{5,4,3,2,1,0:T(8,128)(2,1)S(1)} copy-done((bf16[17,2,2,4,80,128]{5,4,3,2,1,0:T(8,128)(2,1)S(1)}, bf16[17,2,2,4,80,128]{5,4,3,2,1,0:T(8,128)(2,1)}, u32[]{:S(2)}) %copy-start) | copy-done | bytes 5570584
  172.9 0.0 copy-start.1
  172.9 1.1 copy-done.1
  174.0 0.0 copy-start.2
  174.0 1.0 copy-done.2
  174.9 4.6 %finish.1 = (f32[1024,640]{1,0:T(8,128)}, f32[320,2048]{1,0:T(8,128)}, f32[320,2048]{1,0:T(8,128)}, f32[512,640]{1,0:T(8,128)}, f32[320,1024]{1,0:T(8,128)}, /*i...) custom-call(bf16[17,2,2,4,80,128]{5,4,3,2,1,0:T(8,128)(2,1)S(1)} %copy-done, ...), custom_call_target="tpu_custom_call" | custom-call | tf_op jit(solution)/shard_map/finish/pallas_call | solution.py:1009
  (6 shorter events, 0.0 us)
Async XLA Ops:
  170.3 2.6 %copy-start = (bf16[17,2,2,4,80,128]{5,4,3,2,1,0:T(8,128)(2,1)S(1)}, bf16[17,2,2,4,80,128]{5,4,3,2,1,0:T(8,128)(2,1)}, u32[]{:S(2)}) copy-start(bf16[17,2,2,4,80,128]{5,4,3,2,1,0:T(8,128)(2,1)} %get-tuple-element.28.summed) | copy-start | bytes 16711684
  172.9 1.1 copy-start.1
  174.0 1.0 copy-start.2

commit v2 on v1

--- a/solution.py
+++ b/solution.py
@@ -917,17 +917,31 @@
     )(x, cotangent, docs, cos_table, sin_table, gains_own, *weights)
 
 
-def finish_kernel(plan, count, summed, layer_in, inputs_in, *refs):
+def finish_kernel(plan, count, summed_in, layer_in, inputs_in, *refs):
     outs, layer_out, grad_inputs = refs[:count], refs[count], refs[count + 1]
     stages = refs[count + 2 : 2 * count + 2]
-    chunk_sems, side_sems = refs[2 * count + 2 :]
-    depth, rows = summed.shape[3], summed.shape[4]
+    summed, layer_stage, inputs_stage, chunk_sems, side_sems, in_sems = refs[2 * count + 2 :]
+    chunks, depth, rows = summed.shape[0], summed.shape[3], summed.shape[4]
+
+    def fetch(c):
+        return pltpu.make_async_copy(summed_in.at[c], summed.at[c], in_sems.at[c])
+
     sides = [
-        pltpu.make_async_copy(layer_in, layer_out, side_sems.at[0]),
-        pltpu.make_async_copy(inputs_in, grad_inputs, side_sems.at[1]),
+        pltpu.make_async_copy(layer_in, layer_stage, in_sems.at[chunks]),
+        pltpu.make_async_copy(inputs_in, inputs_stage, in_sems.at[chunks + 1]),
     ]
+    puts = [
+        pltpu.make_async_copy(layer_stage, layer_out, side_sems.at[0]),
+        pltpu.make_async_copy(inputs_stage, grad_inputs, side_sems.at[1]),
+    ]
+    fetch(0).start()
     for copy in sides:
         copy.start()
+
+    @pl.loop(1, chunks)
+    def _(c):
+        fetch(c).start()
+
 
     def copies(group, at):
         outputs, by_columns, start, parts = group
@@ -947,6 +961,7 @@
     def convert(group, at):
         outputs, by_columns, start, parts = group
         stage = stages[outputs[0]]
+        fetch(start + at).wait()
         for core in range(2):
             for x in range(2):
                 for z in range(depth):
@@ -976,6 +991,9 @@
         for copy in copies(group, at):
             copy.start()
 
+    for copy, put in zip(sides, puts):
+        copy.wait()
+        put.start()
     for group in plan:
         if group[3] == 1:
             convert(group, 0)
@@ -985,8 +1003,8 @@
         for at in range(group[3]):
             for copy in copies(group, at):
                 copy.wait()
-    for copy in sides:
-        copy.wait()
+    for put in puts:
+        put.wait()
 
 
 def finish(summed, layer_out, grad_inputs, shapes):
@@ -1004,17 +1022,22 @@
         plan.append((list(range(index, index + together)), by_columns, start, parts))
         start += parts
         index += together
-    vmem, anywhere = pl.BlockSpec(memory_space=pltpu.VMEM), pl.BlockSpec(memory_space=pl.ANY)
+    anywhere = pl.BlockSpec(memory_space=pl.ANY)
     results = [jax.ShapeDtypeStruct(shape, jnp.float32) for shape in shapes]
     return pl.pallas_call(
         functools.partial(finish_kernel, plan, len(shapes)),
         out_shape=results
         + [jax.ShapeDtypeStruct(a.shape, a.dtype) for a in (layer_out, grad_inputs)],
-        in_specs=[vmem] * 3,
+        in_specs=[anywhere] * 3,
         out_specs=[anywhere] * (len(shapes) + 2),
         scratch_shapes=[pltpu.VMEM(shape, jnp.float32) for shape in shapes]
-        + [pltpu.SemaphoreType.DMA((chunks + len(shapes),)), pltpu.SemaphoreType.DMA((2,))],
-        compiler_params=pltpu.CompilerParams(vmem_limit_bytes=40 * 2**20),
+        + [pltpu.VMEM(a.shape, a.dtype) for a in (summed, layer_out, grad_inputs)]
+        + [
+            pltpu.SemaphoreType.DMA((chunks + len(shapes),)),
+            pltpu.SemaphoreType.DMA((2,)),
+            pltpu.SemaphoreType.DMA((chunks + 2,)),
+        ],
+        compiler_params=pltpu.CompilerParams(vmem_limit_bytes=67043328),
         name="finish",
     )(summed, layer_out, grad_inputs)
 

time: 180 us -> 177 us (0.983)
  local copies, waits for them, and re-layouts: 4.64 us -> 0 us
  Pallas kernels: 165 us -> 167 us
    unnamed x6 -> x0, local copies, waits for them, and re-layouts: 4.64 us -> none
where the time goes in v2:
time: 177 us
  Pallas kernels  167 us (94%)
  other arithmetic  9.11 us (5%)
    pallas_call x1, Pallas kernels, run_layer(): pl.pallas_call(functools.partial(layer_kernel, tuple(scratch)), out_shape...  160 us
    pallas_call x1, Pallas kernels, finish(): pl.pallas_call(functools.partial(finish_kernel, plan, len(shapes)), out_s...  6.3 us
    convert_element_type x6, other arithmetic, pack_gains(): vec = vec.astype(jnp.float32)  4.04 us

profile of v2, /device:TPU:0, one launch (start us, length us, event | category | flops | bytes accessed | tf_op | source)
XLA Modules:
  0.0 176.6 jit_solution(6082241077362400228)
XLA Ops:
  0.7 0.7 convert_element_type.43
  1.3 0.7 convert_element_type.42
  2.0 0.7 convert_element_type.47
  2.7 0.7 convert_element_type.46
  3.4 0.7 convert_element_type.45
  4.1 0.7 convert_element_type.44
  4.7 0.1 pad_select_fusion.2
  4.8 0.1 pad_select_fusion
  4.9 0.7 select_select_fusion.refs_5_
  5.6 1.2 multiply_sine_fusion
  6.8 160.5 %layer.1 = (bf16[256,640]{1,0:T(8,128)(2,1)}, f32[256,640]{1,0:T(8,128)}, bf16[17,2,2,4,80,128]{5,4,3,2,1,0:T(8,128)(2,1)}, f32[8,640]{1,0:T(8,128)}) custom-call(bf16[256,640]{1,0:T(8,128)(2,1)} %refs_0_.1, bf16[256,640]{1,0:T(8,128)(2,1)} %refs_1_.1, s32[2,128]{1,0:T(2,128)} %bitcast.5, f32[256,128]{1,0:T(8,128)} %get-tuple-element.48.refs_3_, ...), custom_call_target="tpu_custom_call" | custom-call | tf_op jit(solution)/shard_map/layer/pallas_call | solution.py:902
  167.3 1.3 fusion.5
  168.6 1.7 fusion.3
  170.3 6.3 %finish.1 = (f32[1024,640]{1,0:T(8,128)}, f32[320,2048]{1,0:T(8,128)}, f32[320,2048]{1,0:T(8,128)}, f32[512,640]{1,0:T(8,128)}, f32[320,1024]{1,0:T(8,128)}, /*i...) custom-call(bf16[17,2,2,4,80,128]{5,4,3,2,1,0:T(8,128)(2,1)} %get-tuple-element.28.summed_i, ...), custom_call_target="tpu_custom_call" | custom-call | tf_op jit(solution)/shard_map/finish/pallas_call | solution.py:1027
  (6 shorter events, 0.0 us)
